TPU v7x, 32 devices: a whole 2x2x4 slice. The times are simulated.
32 devices in a mesh: dp: 2 (over core), row: 4 (over y, x), col: 4 (over z).
Axes of the slice: x: 2, y: 2, z: 4, core: 2. Of those that a mesh axis runs over, the one named last changes fastest.
Arguments:
- tokens: bfloat16 [1024, 768], P(('dp', 'col'), 'row'), may hold values from -150 to 150
- out_grad: bfloat16 [1024, 768], P(('dp', 'col'), 'row'), may hold values from -6 to 6
- segment_ids: int32 [2, 512], P('dp'), may hold values from 0 to 1, never falling along the last dimension, each value on 1 to 384 neighbouring positions
- w_qkv: bfloat16 [768, 2304], P('row', 'col'), may hold values from -8 to 8
- w_out: bfloat16 [768, 768], P('col', 'row'), may hold values from -0.875 to 0.875
- w_fc: bfloat16 [768, 3072], P('row', 'col'), may hold values from -0.21875 to 0.21875
- w_proj: bfloat16 [3072, 768], P('col', 'row'), may hold values from -0.109375 to 0.109375
- bias_qkv: float32 [2304], P('col'), may hold values from -1.8 to 1.8
- bias_fc: float32 [3072], P('col'), may hold values from -1.8 to 1.8
- row_vectors: float32 [6, 768], P(None, 'row'), may hold values from -0.6 to 1.5
- mom_qkv: float32 [768, 2304], P('row', 'col'), may hold values from -20 to 20
- mom_out: float32 [768, 768], P('col', 'row'), may hold values from -20 to 20
- mom_fc: float32 [768, 3072], P('row', 'col'), may hold values from -20 to 20
- mom_proj: float32 [3072, 768], P('col', 'row'), may hold values from -20 to 20
- mom_bias_qkv: float32 [2304], P('col'), may hold values from -20 to 20
- mom_bias_fc: float32 [3072], P('col'), may hold values from -20 to 20
- mom_rows: float32 [6, 768], P(None, 'row'), may hold values from -20 to 20
Outputs:
- block_out: bfloat16 [1024, 768], P(('dp', 'col'), 'row')
- input_grad: float32 [1024, 768], P(('dp', 'col'), 'row')
- grad_qkv: float32 [768, 2304], P('row', 'col')
- grad_out: float32 [768, 768], P('col', 'row')
- grad_fc: float32 [768, 3072], P('row', 'col')
- grad_proj: float32 [3072, 768], P('col', 'row')
- grad_bias_qkv: float32 [2304], P('col')
- grad_bias_fc: float32 [3072], P('col')
- grad_rows: float32 [6, 768], P(None, 'row')
- new_qkv: float32 [768, 2304], P('row', 'col')
- new_out: float32 [768, 768], P('col', 'row')
- new_fc: float32 [768, 3072], P('row', 'col')
- new_proj: float32 [3072, 768], P('col', 'row')
- new_bias_qkv: float32 [2304], P('col')
- new_bias_fc: float32 [3072], P('col')
- new_rows: float32 [6, 768], P(None, 'row')
- new_mom_qkv: float32 [768, 2304], P('row', 'col')
- new_mom_out: float32 [768, 768], P('col', 'row')
- new_mom_fc: float32 [768, 3072], P('row', 'col')
- new_mom_proj: float32 [3072, 768], P('col', 'row')
- new_mom_bias_qkv: float32 [2304], P('col')
- new_mom_bias_fc: float32 [3072], P('col')
- new_mom_rows: float32 [6, 768], P(None, 'row')
Inputs may be any that keep to these rules, and one draw needn't show every extreme that they name: `segment_ids`: within each data group the segment numbers never fall; the group's 2 sequences have 512 tokens together, each at most 384.
All inputs are finite; a program needn't handle non-finite values.
Results may differ from a plain program's by a relative error of at most 0.012.
Values may be sent and summed in bfloat16 or wider, within the bound.
A program may use at most 128 MiB of HBM per device.

v0:
```python
import functools
import math

import jax
import jax.numpy as jnp
from jax import lax
from jax.experimental import pallas as pl
from jax.experimental.pallas import tpu as pltpu
from jax.sharding import PartitionSpec as P

HD = 64
NS_STEPS = 2


eps_norm = 1e-05
eps_gram = 1e-06
coef_a = 3.4445
coef_b = -4.775
coef_c = 2.0315
beta_mom = 0.95
rate_matrix = 0.03
rate_vector = 0.6


def gelu_value(values):
    return jax.nn.gelu(values, approximate=True)


def gelu_slope(values):
    return jax.vjp(gelu_value, values)[1](jnp.ones_like(values))[0]


def product(left_side, right_side, flip_right):
    if flip_right:
        return lax.dot_general(
            left_side, right_side, (((1,), (1,)), ((), ())), preferred_element_type=jnp.float32
        )
    return jnp.dot(left_side, right_side, preferred_element_type=jnp.float32)


def inner_rows(left_side, right_side):
    return lax.dot_general(
        left_side, right_side, (((0,), (0,)), ((), ())), preferred_element_type=jnp.float32
    )


def exchange_kernel(axes, parts, kinds, *refs):
    count = len(kinds)
    sources, targets = refs[:count], refs[count : 2 * count]
    send_sem, recv_sem, local_sem = refs[2 * count :]
    barrier = pltpu.get_barrier_semaphore()
    met = 0
    for axis in sorted(set(axes)):
        axis_parts = parts[axes.index(axis)]
        for step in range(1, axis_parts):
            peer = lax.rem(lax.axis_index(axis) + step, axis_parts)
            pl.semaphore_signal(
                barrier, inc=1, device_id={axis: peer}, device_id_type=pl.DeviceIdType.MESH
            )
            met += 1
    pl.semaphore_wait(barrier, met)
    copies = []
    for which in range(count):
        axis = axes[which]
        me = lax.axis_index(axis)
        for step in range(1, parts[which]):
            peer = lax.rem(me + step, parts[which])
            copy = pltpu.make_async_remote_copy(
                src_ref=sources[which].at[peer] if kinds[which] else sources[which],
                dst_ref=targets[which].at[me],
                send_sem=send_sem.at[which, step - 1],
                recv_sem=recv_sem.at[which, step - 1],
                device_id={axis: peer},
                device_id_type=pl.DeviceIdType.MESH,
            )
            copy.start()
            copies.append(copy)
    for which in range(count):
        me = lax.axis_index(axes[which])
        copy = pltpu.make_async_copy(
            sources[which].at[me] if kinds[which] else sources[which],
            targets[which].at[me],
            local_sem.at[which],
        )
        copy.start()
        copies.append(copy)
    for copy in copies:
        copy.wait()


def exchange(axes, arrays, kinds, name_id):
    count = len(arrays)
    if isinstance(axes, str):
        axes = [axes] * count
    parts = [lax.axis_size(axis) for axis in axes]
    shapes = [
        jax.ShapeDtypeStruct(array.shape if kind else (part,) + array.shape, array.dtype)
        for array, kind, part in zip(arrays, kinds, parts)
    ]
    return pl.pallas_call(
        functools.partial(exchange_kernel, tuple(axes), tuple(parts), tuple(kinds)),
        out_shape=shapes,
        in_specs=[pl.BlockSpec(memory_space=pltpu.VMEM)] * count,
        out_specs=[pl.BlockSpec(memory_space=pltpu.VMEM)] * count,
        scratch_shapes=[
            pltpu.SemaphoreType.DMA((count, max(parts) - 1)),
            pltpu.SemaphoreType.DMA((count, max(parts) - 1)),
            pltpu.SemaphoreType.DMA((count,)),
        ],
        compiler_params=pltpu.CompilerParams(collective_id=name_id, has_side_effects=True),
    )(*arrays)


def total(slots):
    return jnp.sum(slots.astype(jnp.float32), axis=0)


def side_by_side(slots):
    return jnp.concatenate([slots[part] for part in range(slots.shape[0])], axis=1)


def norm_stats(values):
    mean_row = jnp.mean(values, axis=1, keepdims=True)
    square = jnp.mean(values * values, axis=1, keepdims=True)
    inv_std = lax.rsqrt(square - mean_row * mean_row + eps_norm)
    return mean_row, inv_std


def matrix_product(left_side, right_side):
    return jnp.dot(
        left_side.astype(jnp.bfloat16),
        right_side.astype(jnp.bfloat16),
        preferred_element_type=jnp.float32,
    )


def polynomial_factor(gram_matrix):
    gram_norm = jnp.sqrt(jnp.sum(gram_matrix * gram_matrix)) + eps_gram
    gram_now = gram_matrix / gram_norm
    poly_before = None
    for repeat in range(NS_STEPS):
        poly = coef_b * gram_now + coef_c * matrix_product(gram_now, gram_now)
        if poly_before is None:
            factor = poly
            scale = coef_a
        else:
            factor = coef_a * factor + scale * poly + matrix_product(poly, factor)
            scale = scale * coef_a
        if repeat + 1 < NS_STEPS:
            half = coef_a * gram_now + matrix_product(poly, gram_now)
            gram_now = coef_a * half + matrix_product(half, poly)
        poly_before = poly
    return factor, scale, gram_norm


def local(
    tokens,
    out_grad,
    segment_ids,
    w_qkv,
    w_out,
    w_fc,
    w_proj,
    bias_qkv,
    bias_fc,
    row_vectors,
    mom_qkv,
    mom_out,
    mom_fc,
    mom_proj,
    mom_bias_qkv,
    mom_bias_fc,
    mom_rows,
):
    low = jnp.bfloat16
    score_scale = 1.0 / math.sqrt(HD)
    row_parts = lax.axis_size("row")
    col_parts = lax.axis_size("col")
    dp_parts = lax.axis_size("dp")
    own_tokens, own_features = tokens.shape
    token_count = own_tokens * col_parts
    feature_count = own_features * row_parts
    token_base = lax.axis_index("col") * own_tokens
    feature_base = lax.axis_index("row") * own_features

    def own_columns(whole):
        return lax.dynamic_slice_in_dim(whole, feature_base, own_features, 1)

    def own_block(whole):
        return lax.dynamic_slice(whole, (token_base, feature_base), (own_tokens, own_features))

    def own_rows(whole):
        return lax.dynamic_slice_in_dim(whole, token_base, own_tokens, 0)

    proj_flip = w_proj.T
    tokens_tall, grad_tall, out_tall = exchange(
        "col", [tokens, out_grad, w_out.T], [False] * 3, 0
    )
    grad_cols = grad_tall.reshape(token_count, own_features)
    matrices = [w_qkv, side_by_side(out_tall), w_fc, proj_flip]
    halved = dp_parts == 2
    pieces = matrices
    if halved:
        piece_size = own_features // 2
        pieces = [
            lax.dynamic_slice_in_dim(whole, lax.axis_index("dp") * piece_size, piece_size, 0)
            for whole in matrices
        ]
    token_slots, grad_slots, vector_slots, *gathered = exchange(
        "row",
        [
            tokens_tall.reshape(token_count, own_features),
            grad_cols.reshape(row_parts, -1, own_features),
            row_vectors,
        ]
        + pieces,
        [False, True, False] + [False] * 4,
        1,
    )
    if halved:
        gathered = [
            both.transpose(1, 0, 2, 3)
            for both in exchange("dp", gathered, [False] * 4, 19)
        ]
    qkv_cols, out_flip, fc_cols, proj_cols = [
        slots.reshape(feature_count, -1) for slots in gathered
    ]
    tokens_all = side_by_side(token_slots)
    grad_part = side_by_side(grad_slots)
    vectors_all = side_by_side(vector_slots)
    gain_one, shift_one, gain_two, shift_two, bias_out, _ = [
        vectors_all[which] for which in range(6)
    ]

    resid_in = tokens_all.astype(jnp.float32)
    mean_one, inv_one = norm_stats(resid_in)
    unit_one = (resid_in - mean_one) * inv_one
    act_one = (unit_one * gain_one + shift_one).astype(low)
    qkv_local = (product(act_one, qkv_cols, False) + bias_qkv).astype(low)
    heads_local = qkv_local.shape[1] // (3 * HD)
    qkv_tiles = qkv_local.reshape(token_count, heads_local, 3, HD).transpose(2, 1, 0, 3)
    query, key, value = qkv_tiles[0], qkv_tiles[1], qkv_tiles[2]
    segment_row = segment_ids[0]
    positions = jnp.arange(token_count, dtype=jnp.int32)
    allowed = (positions[None, :] <= positions[:, None]) & (
        segment_row[None, :] == segment_row[:, None]
    )
    scores = (
        jnp.einsum("hqe,hke->hqk", query, key, preferred_element_type=jnp.float32) * score_scale
    )
    scores = jnp.where(allowed[None], scores, -jnp.inf)
    row_max = jnp.max(scores, axis=2, keepdims=True)
    raised = jnp.exp(scores - row_max)
    probs = raised / jnp.sum(raised, axis=2, keepdims=True)
    prob_low = probs.astype(low)
    attended = jnp.einsum(
        "hqk,hke->hqe", prob_low, value, preferred_element_type=jnp.float32
    ).astype(low)
    attn_local = attended.transpose(1, 0, 2).reshape(token_count, heads_local * HD)
    part_tokens = token_count // row_parts
    part_base = lax.axis_index("row") * part_tokens

    def part_rows(whole):
        return lax.dynamic_slice_in_dim(whole, part_base, part_tokens, 0)

    (attn_slots,) = exchange("col", [part_rows(attn_local)], [False], 2)
    attn_part = jnp.concatenate([attn_slots[part] for part in range(col_parts)], axis=1)
    resid_mid = part_rows(resid_in) + product(attn_part, out_flip, True) + bias_out
    mean_two, inv_two = norm_stats(resid_mid)
    unit_two = (resid_mid - mean_two) * inv_two
    act_two = (unit_two * gain_two + shift_two).astype(low)
    hidden_pre = product(act_two, fc_cols, False) + bias_fc
    hidden = gelu_value(hidden_pre).astype(low)
    grad_hidden = product(grad_part, proj_cols, False)
    grad_pre = (gelu_slope(hidden_pre) * grad_hidden).astype(low)

    piece_tokens = part_tokens // col_parts
    piece_base = lax.axis_index("col") * piece_tokens

    def piece_rows(part):
        return lax.dynamic_slice_in_dim(part, piece_base, piece_tokens, 0)

    (two_slots,) = exchange(
        "col",
        [product(grad_pre, fc_cols, True).astype(low).reshape(col_parts, piece_tokens, -1)],
        [True],
        3,
    )
    grad_norm_two = total(two_slots)
    unit_two_piece = piece_rows(unit_two)
    scaled = grad_norm_two * gain_two
    first_mean = jnp.mean(scaled, axis=1, keepdims=True)
    second_mean = jnp.mean(scaled * unit_two_piece, axis=1, keepdims=True)
    grad_mid_piece = piece_rows(grad_part).astype(jnp.float32) + piece_rows(inv_two) * (
        scaled - first_mean - unit_two_piece * second_mean
    )
    grad_mid_low = grad_mid_piece.astype(low)
    (mid_slots,) = exchange("col", [grad_mid_low], [False], 4)
    mid_part = mid_slots.reshape(part_tokens, feature_count)
    out_rows = lax.dynamic_slice_in_dim(
        out_flip, lax.axis_index("col") * w_out.shape[0], w_out.shape[0], 1
    )
    grad_attn_part = product(mid_part, out_rows, False).astype(low)
    split = lambda rows: rows.reshape(part_tokens, row_parts, own_features).transpose(1, 0, 2)
    attn_grad_slots, mid_cols, act_two_cols, hidden_slots, grad_pre_slots, resid_cols = exchange(
        "row",
        [
            grad_attn_part,
            split(mid_part),
            split(act_two),
            hidden,
            grad_pre,
            split(resid_mid),
        ],
        [False, True, True, False, False, True],
        5,
    )
    grad_attn = (
        attn_grad_slots.reshape(token_count, heads_local, HD).transpose(1, 0, 2)
    )
    mid_cols = mid_cols.reshape(token_count, own_features)
    act_two_cols = act_two_cols.reshape(token_count, own_features)
    resid_cols = resid_cols.reshape(token_count, own_features)
    hidden_all = hidden_slots.reshape(token_count, -1)
    grad_pre_all = grad_pre_slots.reshape(token_count, -1)

    grad_value = jnp.einsum(
        "hqk,hqe->hke", prob_low, grad_attn, preferred_element_type=jnp.float32
    )
    grad_probs = jnp.einsum("hqe,hke->hqk", grad_attn, value, preferred_element_type=jnp.float32)
    row_dot = jnp.sum(
        grad_attn.astype(jnp.float32) * attended.astype(jnp.float32), axis=2, keepdims=True
    )
    grad_scores = (score_scale * probs * (grad_probs - row_dot)).astype(low)
    grad_query = jnp.einsum("hqk,hke->hqe", grad_scores, key, preferred_element_type=jnp.float32)
    grad_key = jnp.einsum("hqk,hqe->hke", grad_scores, query, preferred_element_type=jnp.float32)
    grad_qkv_low = (
        jnp.stack([grad_query.astype(low), grad_key.astype(low), grad_value.astype(low)], axis=0)
        .transpose(2, 1, 0, 3)
        .reshape(token_count, heads_local * 3 * HD)
    )

    grad_blocks = (
        inner_rows(own_columns(act_one), grad_qkv_low),
        inner_rows(attn_local, mid_cols),
        inner_rows(act_two_cols, grad_pre_all),
        inner_rows(hidden_all, grad_cols),
    )
    bias_blocks = jnp.concatenate(
        [
            jnp.sum(grad_qkv_low, axis=0, dtype=jnp.float32),
            jnp.sum(grad_pre_all, axis=0, dtype=jnp.float32),
        ]
    )[None]
    if dp_parts == 2:
        group_slots = exchange(
            "dp", [block.astype(low) for block in grad_blocks] + [bias_blocks], [False] * 5, 6
        )
        summed = [total(slots) for slots in group_slots]
    else:
        summed = [lax.psum(block.astype(low), "dp").astype(jnp.float32) for block in grad_blocks]
        summed.append(lax.psum(bias_blocks, "dp"))
    bias_sums = summed.pop()[0]
    summed = summed + [bias_sums[: bias_qkv.shape[0]], bias_sums[bias_qkv.shape[0] :]]

    weights = (w_qkv, w_out, w_fc, w_proj)
    moments = (mom_qkv, mom_out, mom_fc, mom_proj)
    flips = (False, True, False, True)
    new_moms = [beta_mom * moments[member] + summed[member] for member in range(4)]
    pushes = [
        (summed[member] + beta_mom * new_moms[member]).astype(low) for member in range(4)
    ]
    upright = [pushes[member].T if flips[member] else pushes[member] for member in range(4)]
    widest = max(piece.shape[1] for piece in upright)
    share = -(-widest // dp_parts)
    assert row_parts == len(upright)
    outgoing = jnp.stack(
        [
            jnp.pad(piece, ((0, 0), (0, share * dp_parts - piece.shape[1])))
            for piece in upright
        ]
    )
    outgoing = lax.dynamic_slice_in_dim(outgoing, lax.axis_index("dp") * share, share, 2)
    outward = product(hidden_all, proj_flip, True).astype(low)
    inward = product(grad_qkv_low, w_qkv, True).astype(low)
    arrived, block_slots, one_slots = exchange(
        ["row", "col", "col"],
        [
            outgoing,
            outward.reshape(col_parts, own_tokens, own_features),
            inward.reshape(col_parts, own_tokens, own_features),
        ],
        [True] * 3,
        7,
    )
    matrix = arrived.reshape(feature_count, share)
    gram_low = product(matrix, matrix, True).astype(low)
    edge = feature_count // 3
    spots = [(0, 0), (0, 1), (0, 2), (1, 1), (1, 2), (2, 2)]
    packed = jnp.concatenate(
        [
            gram_low[up * edge : (up + 1) * edge, across * edge : (across + 1) * edge]
            for up, across in spots
        ],
        axis=0,
    )
    block_out = (own_rows(resid_cols) + total(block_slots) + row_vectors[5]).astype(low)
    grad_norm_one = total(one_slots)
    unit_one_own = own_block(unit_one)
    scaled_one = grad_norm_one * row_vectors[0]
    stat_pair = jnp.stack(
        [jnp.sum(scaled_one, axis=1), jnp.sum(scaled_one * unit_one_own, axis=1)]
    )
    wide_terms = jnp.stack(
        [
            jnp.sum(grad_norm_two * unit_two_piece, axis=0),
            jnp.sum(grad_norm_two, axis=0),
        ]
    )
    wide_slot_terms = wide_terms.reshape(2, row_parts, own_features).transpose(1, 0, 2)
    if dp_parts == 2:
        stat_slots, wide_slots, half_slots = exchange(
            ["row", "row", "dp"],
            [stat_pair, wide_slot_terms, packed.reshape(dp_parts, -1, edge)],
            [False, True, True],
            8,
        )
        gram_half = total(half_slots).astype(low)
    else:
        stat_slots, wide_slots = exchange(
            "row", [stat_pair, wide_slot_terms], [False, True], 8
        )
        gram_half = lax.psum(packed, "dp")
    stat_sum = total(stat_slots)
    first_sum, second_sum = stat_sum[0][:, None], stat_sum[1][:, None]
    wide_sum = total(wide_slots)
    input_grad = own_rows(mid_cols).astype(jnp.float32) + own_rows(inv_one) * (
        scaled_one - first_sum / feature_count - unit_one_own * (second_sum / feature_count)
    )
    row_terms = jnp.stack(
        [
            jnp.sum(grad_norm_one * unit_one_own, axis=0),
            jnp.sum(grad_norm_one, axis=0),
            wide_sum[0],
            wide_sum[1],
            jnp.sum(own_rows(mid_cols), axis=0, dtype=jnp.float32),
            jnp.sum(out_grad, axis=0, dtype=jnp.float32),
        ]
    )
    quarter_slots, term_slots = exchange(
        "col",
        [gram_half.reshape(col_parts, -1, edge), row_terms],
        [True, False],
        9,
    )
    (whole_slots,) = exchange("col", [total(quarter_slots).astype(low)], [False], 10)
    gram_half = whole_slots.reshape(gram_half.shape)
    if dp_parts == 2:
        gram_slots, pair_slots = exchange(
            "dp", [gram_half, total(term_slots)], [False, False], 11
        )
        gram_half = gram_slots
    else:
        (pair_slots,) = exchange("dp", [total(term_slots)], [False], 11)
    grad_rows = total(pair_slots)
    tiles = gram_half.reshape(len(spots), edge, edge)
    found = {spot: tiles[which] for which, spot in enumerate(spots)}
    gram = jnp.concatenate(
        [
            jnp.concatenate(
                [
                    found[up, across] if across >= up else found[across, up].T
                    for across in range(3)
                ],
                axis=1,
            )
            for up in range(3)
        ],
        axis=0,
    ).astype(jnp.float32)
    factor, scale, gram_norm = polynomial_factor(gram)
    ortho = (scale * matrix.astype(jnp.float32) + matrix_product(factor, matrix)) * lax.rsqrt(
        gram_norm
    )
    (back,) = exchange(
        "row", [ortho.astype(low).reshape(row_parts, own_features, share)], [True], 12
    )
    if dp_parts == 2:
        (ortho_slots,) = exchange("dp", [back], [False], 13)
        orthos = jnp.concatenate([ortho_slots[part] for part in range(dp_parts)], axis=2)
    else:
        orthos = lax.all_gather(back, "dp", axis=2, tiled=True)
    new_weights = []
    for member in range(4):
        piece = orthos[member, :, : upright[member].shape[1]]
        if flips[member]:
            piece = piece.T
        longest = max(
            upright[member].shape[0] * row_parts, upright[member].shape[1] * col_parts
        )
        new_weights.append(
            weights[member].astype(jnp.float32)
            - rate_matrix * math.sqrt(longest) * piece.astype(jnp.float32)
        )

    vector_rate = rate_vector / math.sqrt(token_count * dp_parts)

    def vector_step(weight, gradient, moment):
        new_moment = beta_mom * moment + gradient
        return (weight - vector_rate * (gradient + beta_mom * new_moment), new_moment)

    new_bias_qkv, new_mom_bias_qkv = vector_step(bias_qkv, summed[4], mom_bias_qkv)
    new_bias_fc, new_mom_bias_fc = vector_step(bias_fc, summed[5], mom_bias_fc)
    new_rows, new_mom_rows = vector_step(row_vectors, grad_rows, mom_rows)
    return (
        block_out,
        input_grad,
        summed[0],
        summed[1],
        summed[2],
        summed[3],
        summed[4],
        summed[5],
        grad_rows,
        new_weights[0],
        new_weights[1],
        new_weights[2],
        new_weights[3],
        new_bias_qkv,
        new_bias_fc,
        new_rows,
        new_moms[0],
        new_moms[1],
        new_moms[2],
        new_moms[3],
        new_mom_bias_qkv,
        new_mom_bias_fc,
        new_mom_rows,
    )


def solution(mesh):
    placed = (
        P(("dp", "col"), "row"),
        P(("dp", "col"), "row"),
        P("dp", None),
        P("row", "col"),
        P("col", "row"),
        P("row", "col"),
        P("col", "row"),
        P("col"),
        P("col"),
        P(None, "row"),
        P("row", "col"),
        P("col", "row"),
        P("row", "col"),
        P("col", "row"),
        P("col"),
        P("col"),
        P(None, "row"),
    )
    return jax.shard_map(
        local,
        mesh=mesh,
        in_specs=placed,
        out_specs=(
            P(("dp", "col"), "row"),
            P(("dp", "col"), "row"),
            P("row", "col"),
            P("col", "row"),
            P("row", "col"),
            P("col", "row"),
            P("col"),
            P("col"),
            P(None, "row"),
            P("row", "col"),
            P("col", "row"),
            P("row", "col"),
            P("col", "row"),
            P("col"),
            P("col"),
            P(None, "row"),
            P("row", "col"),
            P("col", "row"),
            P("row", "col"),
            P("col", "row"),
            P("col"),
            P("col"),
            P(None, "row"),
        ),
        check_vma=False,
    )
```

profile of v0, /device:TPU:25, one launch (start us, length us, event | category | flops | bytes accessed | tf_op | source)
XLA Modules:
  0.0 348.1 jit_solution(11143103750796626464)
XLA Ops:
  13.5 24.0 %shard_map.347 = (bf16[4,128,192]{2,1,0:T(8,128)(2,1)}, bf16[4,128,192]{2,1,0:T(8,128)(2,1)}, bf16[4,192,192]{2,1,0:T(8,128)(2,1)}) custom-call(bf16[128,192]{1,0:T(8,128)(2,1)} %copy.196.refs_0_, bf16[128,192]{1,0:T(8,128)(2,1)} %copy.197.refs_1_, bf16[192,192]{1,0:T(8,128)(2,1)} %bitcast.260), custom_call_target="tpu_custom_call" | custom-call | tf_op jit(solution)/shard_map/pallas_call | solution.py:100
  39.3 45.7 %shard_map.348 = (bf16[4,512,192]{2,1,0:T(8,128)(2,1)}, bf16[4,128,192]{2,1,0:T(8,128)(2,1)}, f32[4,6,192]{2,1,0:T(8,128)}, bf16[4,96,576]{2,1,0:T(8,128)(2,1)},...) custom-call(bf16[512,192]{1,0:T(8,128)(2,1)} %bitcast.269, ...), custom_call_target="tpu_custom_call" | custom-call | tf_op jit(solution)/shard_map/pallas_call | solution.py:100
  92.5 8.9 %shard_map.349 = (bf16[2,4,96,576]{3,2,1,0:T(8,128)(2,1)}, bf16[2,4,96,768]{3,2,1,0:T(8,128)(2,1)}, bf16[2,4,96,768]{3,2,1,0:T(8,128)(2,1)}, bf16[2,4,96,768]{3,2,1,0:T(8,128)(2,1)}) custom-call(bf16[4,96,576]{2,1,0:T(8,128)(2,1)} %get-tuple-element.64.refs_0_, bf16[4,96,768]{2,1,0:T(8,128)(2,1)} %get-tuple-element.65.refs_1_, ...), custom_call_target="tpu_custom_call" | custom-call | tf_op jit(solution)/shard_map/pallas_call | solution.py:100
  107.5 2.9 fusion.71
  111.0 2.3 fusion.10
  115.9 9.2 %shard_map.350 = bf16[4,128,192]{2,1,0:T(8,128)(2,1)} custom-call(bf16[128,192]{1,0:T(8,128)(2,1)} %copy.246.refs_0_), custom_call_target="tpu_custom_call" | custom-call | tf_op jit(solution)/shard_map/pallas_call | solution.py:100
  126.1 2.7 fusion.67
  130.3 1.9 copy.208
  132.2 2.0 copy.209
  134.2 1.9 add_convert_fusion.4
  136.2 1.7 copy.206
  137.9 1.8 copy.207
  139.7 2.1 multiply_convert_fusion.1
  143.5 7.6 %shard_map.351 = bf16[4,32,768]{2,1,0:T(8,128)(2,1)} custom-call(bf16[4,32,768]{2,1,0:T(8,128)(2,1)} %bitcast.261), custom_call_target="tpu_custom_call" | custom-call | tf_op jit(solution)/shard_map/pallas_call | solution.py:100
  155.5 7.3 %shard_map.352 = bf16[4,32,768]{2,1,0:T(8,128)(2,1)} custom-call(bf16[32,768]{1,0:T(8,128)(2,1)} %add_convert_fusion.7.refs_0_), custom_call_target="tpu_custom_call" | custom-call | tf_op jit(solution)/shard_map/pallas_call | solution.py:100
  167.1 34.3 %shard_map.353 = (bf16[4,128,192]{2,1,0:T(8,128)(2,1)}, bf16[4,128,192]{2,1,0:T(8,128)(2,1)}, bf16[4,128,192]{2,1,0:T(8,128)(2,1)}, bf16[4,128,768]{2,1,0:T(8,12...) custom-call(bf16[128,192]{1,0:T(8,128)(2,1)} %copy.210.refs_0_, bf16[4,128,192]{2,1,0:T(8,128)(2,1)} %bitcast.257, ...), custom_call_target="tpu_custom_call" | custom-call | tf_op jit(solution)/shard_map/pallas_call | solution.py:100
  202.8 2.3 fusion.11.refs_2_
  206.4 1.8 convolution_convert_fusion.9.refs_1_
  210.1 2.6 multiply_convert_fusion
  215.9 2.3 convolution_convert_fusion.1.refs_0_
  219.4 9.1 %shard_map.354 = (bf16[2,192,576]{2,1,0:T(8,128)(2,1)}, bf16[2,192,192]{2,1,0:T(8,128)(2,1)}, bf16[2,192,768]{2,1,0:T(8,128)(2,1)}, bf16[2,768,192]{2,1,0:T(8,128)(2,1)}, f32[2,1,1344]{2,1,0:T(1,128)}) custom-call(bf16[192,576]{1,0:T(8,128)(2,1)} %convolution_convert_fusion.1.refs_0_, bf16[192,192]{1,0:T(8,128)(2,1)} %convolution_convert_fusion.9.refs_1_, ...), custom_call_target="tpu_custom_call" | custom-call | tf_op jit(solution)/shard_map/pallas_call | solution.py:100
  239.5 16.1 %shard_map.355 = (bf16[4,192,384]{2,1,0:T(8,128)(2,1)}, bf16[4,128,192]{2,1,0:T(8,128)(2,1)}, bf16[4,128,192]{2,1,0:T(8,128)(2,1)}) custom-call(bf16[4,192,384]{2,1,0:T(8,128)(2,1)} %fusion.29.refs_0_, bf16[4,128,192]{2,1,0:T(8,128)(2,1)} %bitcast.254, bf16[4,128,192]{2,1,0:T(8,128)(2,1)} %bitcast.255), custom_call_target="tpu_custom_call" | custom-call | tf_op jit(solution)/shard_map/pallas_call | solution.py:100
  263.0 7.2 %shard_map.356 = (f32[4,2,128]{2,1,0:T(2,128)}, f32[4,2,192]{2,1,0:T(2,128)}, bf16[2,768,256]{2,1,0:T(8,128)(2,1)}) custom-call(f32[2,128]{1,0:T(2,128)} %pad_maximum_fusion.8.refs_0_, f32[4,2,192]{2,1,0:T(2,128)} %maximum_bitcast_fusion.1.refs_1_, bf16[2,768,256]{2,1,0:T(8,128)(2,1)} %bitcast.253), custom_call_target="tpu_custom_call" | custom-call | tf_op jit(solution)/shard_map/pallas_call | solution.py:100
  274.2 2.1 reduce_sum.332
  276.3 11.4 %shard_map.357 = (bf16[4,192,256]{2,1,0:T(8,128)(2,1)}, f32[4,6,192]{2,1,0:T(8,128)}) custom-call(bf16[4,192,256]{2,1,0:T(8,128)(2,1)} %bitcast.239, f32[6,192]{1,0:T(8,128)} %stack.79.refs_1_), custom_call_target="tpu_custom_call" | custom-call | tf_op jit(solution)/shard_map/pallas_call | solution.py:100
  290.8 13.8 %shard_map.358 = bf16[4,192,256]{2,1,0:T(8,128)(2,1)} custom-call(bf16[192,256]{1,0:T(8,128)(2,1)} %reduce_sum.338.refs_0_), custom_call_target="tpu_custom_call" | custom-call | tf_op jit(solution)/shard_map/pallas_call | solution.py:100
  304.6 5.4 %shard_map.359 = (bf16[2,768,256]{2,1,0:T(8,128)(2,1)}, f32[2,6,192]{2,1,0:T(8,128)}) custom-call(bf16[768,256]{1,0:T(8,128)(2,1)} %bitcast.240, f32[6,192]{1,0:T(8,128)} %reduce_sum.339.refs_1_), custom_call_target="tpu_custom_call" | custom-call | tf_op jit(solution)/shard_map/pallas_call | solution.py:100
  315.3 2.9 multiply_add_fusion.4
  320.5 2.5 multiply_add_fusion.1
  323.1 4.9 %fusion.9 = bf16[768,384]{1,0:T(8,128)(2,1)} fusion(bf16[768,384]{1,0:T(8,128)(2,1)S(1)} %bitcast.226, f32[768,768]{1,0:T(8,128)S(1)} %multiply_add_fusion.4, f32[768,768]{1,0:T(8,128)} %multiply_add_fusion.1, f32[]{:T(128)S(6)} %rsqrt.35), kind=kOutput, calls=%fused_computation.28 | convolution fusion | flops 1363968000 | bytes 5898244 | tf_op jit(solution)/shard_map/dot_general | solution.py:130
  328.0 10.2 %shard_map.360.refs_0_ = bf16[4,192,384]{2,1,0:T(8,128)(2,1)} custom-call(bf16[4,192,384]{2,1,0:T(8,128)(2,1)} %bitcast.264), custom_call_target="tpu_custom_call" | custom-call | tf_op jit(solution)/shard_map/pallas_call | solution.py:100
  338.2 5.0 %shard_map.361 = bf16[2,4,192,384]{3,2,1,0:T(8,128)(2,1)} custom-call(bf16[4,192,384]{2,1,0:T(8,128)(2,1)} %shard_map.360.refs_0_), custom_call_target="tpu_custom_call" | custom-call | tf_op jit(solution)/shard_map/pallas_call | solution.py:100
  (233 shorter events, 89.8 us)
Async XLA Ops:
  0.7 37.9 %copy-start.24 = (bf16[192,768]{1,0:T(8,128)(2,1)S(1)}, bf16[192,768]{1,0:T(8,128)(2,1)}, u32[]{:S(2)}) copy-start(bf16[192,768]{1,0:T(8,128)(2,1)} %param.22) | copy-start | bytes 884740
  85.1 3.4 copy-start.17
  92.5 10.2 %copy-start.9 = (bf16[512,768]{1,0:T(8,128)(2,1)}, bf16[512,768]{1,0:T(8,128)(2,1)S(1)}, u32[]{:S(2)}) copy-start(bf16[512,768]{1,0:T(8,128)(2,1)S(1)} %get-tuple-element.251) | copy-start | bytes 2359300
  92.5 10.2 %copy-start.46 = (f32[576]{0:T(1024)S(1)}, f32[576]{0:T(1024)}, u32[]{:S(2)}) copy-start(f32[576]{0:T(1024)} %param.24) | copy-start | bytes 6916
  139.7 2.1 copy-start.38
  142.3 11.6 %copy-start.52 = (f32[32]{0:T(128)S(1)}, f32[32]{0:T(128)}, u32[]{:S(2)}) copy-start(f32[32]{0:T(128)} %dynamic-slice.4) | copy-start | bytes 388
  201.4 3.7 %copy-start = (bf16[4,128,768]{2,1,0:T(8,128)(2,1)S(1)}, bf16[4,128,768]{2,1,0:T(8,128)(2,1)}, u32[]{:S(2)}) copy-start(bf16[4,128,768]{2,1,0:T(8,128)(2,1)} %get-tuple-element.77) | copy-start | bytes 2359300
  201.4 3.7 %copy-start.18 = (bf16[4,128,192]{2,1,0:T(8,128)(2,1)S(1)}, bf16[4,128,192]{2,1,0:T(8,128)(2,1)}, u32[]{:S(2)}) copy-start(bf16[4,128,192]{2,1,0:T(8,128)(2,1)} %get-tuple-element.59.refs_1_) | copy-start | bytes 589828
  215.0 3.2 copy-start.7
  218.2 12.5 %copy-start.47 = (f32[576]{0:T(1024)S(1)}, f32[576]{0:T(1024)}, u32[]{:S(2)}) copy-start(f32[576]{0:T(1024)} %param.24) | copy-start | bytes 6916
  218.2 12.5 %copy-start.48 = (f32[576]{0:T(1024)S(1)}, f32[576]{0:T(1024)}, u32[]{:S(2)}) copy-start(f32[576]{0:T(1024)} %param.31) | copy-start | bytes 6916
  218.2 13.1 %copy-start.49 = (f32[768]{0:T(1024)S(1)}, f32[768]{0:T(1024)}, u32[]{:S(2)}) copy-start(f32[768]{0:T(1024)} %param.25) | copy-start | bytes 9220
  218.2 13.1 %copy-start.50 = (f32[768]{0:T(1024)S(1)}, f32[768]{0:T(1024)}, u32[]{:S(2)}) copy-start(f32[768]{0:T(1024)} %param.32) | copy-start | bytes 9220
  218.5 14.5 %copy-start.22 = (f32[192,192]{0,1:T(8,128)S(1)}, f32[192,192]{0,1:T(8,128)}, u32[]{:S(2)}) copy-start(f32[192,192]{0,1:T(8,128)} %copy.221) | copy-start | bytes 442372
  228.5 5.4 %copy-start.26 = (bf16[2,192,768]{2,1,0:T(8,128)(2,1)S(1)}, bf16[2,192,768]{2,1,0:T(8,128)(2,1)}, u32[]{:S(2)}) copy-start(bf16[2,192,768]{2,1,0:T(8,128)(2,1)} %get-tuple-element.80) | copy-start | bytes 1769476
  229.7 4.3 %copy-start.4 = (f32[192,576]{1,0:T(8,128)}, f32[192,576]{1,0:T(8,128)S(1)}, u32[]{:S(2)}) copy-start(f32[192,576]{1,0:T(8,128)S(1)} %convert_reduce_fusion.5) | copy-start | bytes 1327108
  230.6 3.4 copy-start.41
  230.6 3.4 copy-start.42
  234.0 3.2 copy-start.2
  236.3 2.4 copy-start.3
  255.7 5.5 %copy-start.1 = (bf16[4,192,384]{2,1,0:T(8,128)(2,1)S(1)}, bf16[4,192,384]{2,1,0:T(8,128)(2,1)}, u32[]{:S(2)}) copy-start(bf16[4,192,384]{2,1,0:T(8,128)(2,1)} %get-tuple-element.84) | copy-start | bytes 1769476
  262.0 9.0 %copy-start.53 = (f32[128]{0:T(128)S(1)}, f32[128]{0:T(128)}, u32[]{:S(2)}) copy-start(f32[128]{0:T(128)} %dynamic-slice.5) | copy-start | bytes 1540
  262.0 10.8 %copy-start.45 = (f32[192]{0:T(256)S(1)}, f32[192]{0:T(256)}, u32[]{:S(2)}) copy-start(f32[192]{0:T(256)} %convert_reduce_fusion.13) | copy-start | bytes 2308
  274.2 36.6 %copy-start.39 = (f32[6,192]{1,0:T(8,128)S(1)}, f32[6,192]{1,0:T(8,128)}, u32[]{:S(2)}) copy-start(f32[6,192]{1,0:T(8,128)} %refs_2_.1) | copy-start | bytes 13828
  274.2 36.6 %copy-start.44 = (f32[6,192]{1,0:T(8,128)S(1)}, f32[6,192]{1,0:T(8,128)}, u32[]{:S(2)}) copy-start(f32[6,192]{1,0:T(8,128)} %param.33) | copy-start | bytes 13828
  310.8 2.4 copy-start.40
  315.3 2.9 copy-start.15
  315.3 2.9 copy-start.30
  315.3 2.9 copy-start.32
  315.3 2.9 copy-start.34
  315.3 2.9 copy-start.36
  343.2 2.3 copy-start.8
  (22 other events, 31.3 us)
where the time goes:
time: 353 us; the launch traced here: 348 us
  Pallas kernels  215 us (61%)
  local copies, waits for them, and re-layouts  48.9 us (14%)
  other arithmetic  44.6 us (13%)
  matrix products  37 us (10%)
    pallas_call x15, Pallas kernels, exchange(): pl.pallas_call(functools.partial(exchange_kernel, tuple(axes), tuple(part...  215 us
    unnamed x126, local copies, waits for them, and re-layouts  18 us
    dot_general x5, matrix products, matrix_product(): jnp.dot(left_side.astype(jnp.bfloat16), right_side.astype(jnp.bfloat16),...  12.6 us
    reduce_sum x12, other arithmetic, total(): return jnp.sum(slots.astype(jnp.float32), axis=0)  11.6 us

commit v1 on v0

--- a/solution.py
+++ b/solution.py
@@ -153,6 +153,488 @@
     return factor, scale, gram_norm
 
 
+def contract(left_side, right_side, left_dim, right_dim):
+    return lax.dot_general(
+        left_side,
+        right_side,
+        (((left_dim,), (right_dim,)), ((), ())),
+        preferred_element_type=jnp.float32,
+    )
+
+
+def column_of(row_values):
+    size = row_values.shape[1]
+    up = lax.broadcasted_iota(jnp.int32, (size, size), 0)
+    across = lax.broadcasted_iota(jnp.int32, (size, size), 1)
+    return jnp.sum(jnp.where(up == across, row_values, 0.0), axis=1, keepdims=True)
+
+
+class Wire:
+    def __init__(self, send_sem, recv_sem):
+        self.send_sem, self.recv_sem = send_sem, recv_sem
+        self.used = 0
+        self.live = []
+
+    def push(self, source, target, axis, peer):
+        copy = pltpu.make_async_remote_copy(
+            src_ref=source,
+            dst_ref=target,
+            send_sem=self.send_sem.at[self.used],
+            recv_sem=self.recv_sem.at[self.used],
+            device_id={axis: peer},
+            device_id_type=pl.DeviceIdType.MESH,
+        )
+        self.used += 1
+        copy.start()
+        self.live.append(copy)
+        return copy
+
+    def spread(self, axis, source_of, target_of):
+        parts = lax.axis_size(axis)
+        me = lax.axis_index(axis)
+        copies = []
+        for step in range(1, parts):
+            peer = lax.rem(me + step, parts)
+            copies.append(self.push(source_of(peer), target_of(peer), axis, peer))
+        return copies
+
+    def drain(self):
+        for copy in self.live:
+            copy.wait_send()
+
+
+def greet(axes):
+    barrier = pltpu.get_barrier_semaphore()
+    met = 0
+    for axis in axes:
+        parts = lax.axis_size(axis)
+        for step in range(1, parts):
+            peer = lax.rem(lax.axis_index(axis) + step, parts)
+            pl.semaphore_signal(
+                barrier, inc=1, device_id={axis: peer}, device_id_type=pl.DeviceIdType.MESH
+            )
+            met += 1
+    pl.semaphore_wait(barrier, met)
+
+
+def arrived(copies):
+    for copy in copies:
+        copy.wait_recv()
+
+
+def rows_at(index, size):
+    return pl.ds(pl.multiple_of(index * size, size), size)
+
+
+front_wires = 110
+
+
+def front_kernel(*refs):
+    low, wide = jnp.bfloat16, jnp.float32
+    (
+        tok_in, grad_in, seg_row, wq_in, wo_in, wf_in, wp_in, bias_q, bias_f, vec_in,
+        sum_q, sum_o, sum_f, sum_p, sum_bq, sum_bf, outward, inward, unit_own, inv_own,
+        mid_own, resid_own, wide_out,
+        tok, grad_cols, grad_part, vecs, wq, wo, wf, wp, act_one, qkv, bias_col, mask, probs,
+        attn, attn_part, unit_two, inv_two, act_two, act_cols, mid, hid, gpre, two_out, two_in,
+        gm_piece, mid_part, mid_cols, gattn, gqkv, acc_k, acc_v, mean_one, inv_one,
+        send_sem, recv_sem, local_sem,
+    ) = refs
+    rows, cols = lax.axis_size("row"), lax.axis_size("col")
+    me_r, me_c, me_d = lax.axis_index("row"), lax.axis_index("col"), lax.axis_index("dp")
+    count, feats = tok.shape[1], tok.shape[2]
+    whole = feats * rows
+    block = count // cols
+    piece = block // cols
+    half = feats // 2
+    heads = qkv.shape[0] // (3 * HD)
+    score_scale = 1.0 / math.sqrt(HD)
+    own = rows_at(me_c, block)
+    part = rows_at(me_r, block)
+    bit = rows_at(me_c, piece)
+    wire = Wire(send_sem, recv_sem)
+    locals_ = []
+    for which, (source, target) in enumerate(
+        [
+            (tok_in, tok.at[me_r, own]),
+            (vec_in, vecs.at[me_r]),
+            (wq_in, wq.at[me_r]),
+            (grad_in, grad_cols.at[own]),
+            (wo_in, wo.at[me_c, me_r]),
+            (wf_in, wf.at[me_r]),
+            (wp_in, wp.at[me_r]),
+        ]
+    ):
+        copy = pltpu.make_async_copy(source, target, local_sem.at[which])
+        copy.start()
+        locals_.append(copy)
+    greet(("row", "col", "dp"))
+
+    def halves(size):
+        return rows_at(me_d, size // 2)
+
+    locals_[0].wait()
+    tok_z = wire.spread("col", lambda p: tok.at[me_r, own], lambda p: tok.at[me_r, own])
+    tok_r = [wire.spread("row", lambda p: tok.at[me_r, own], lambda p: tok.at[me_r, own])]
+    locals_[1].wait()
+    vec_r = wire.spread("row", lambda p: vecs.at[me_r], lambda p: vecs.at[me_r])
+    locals_[2].wait()
+    wq_half = halves(wq.shape[1])
+    wq_r = wire.spread("row", lambda p: wq.at[me_r, wq_half], lambda p: wq.at[me_r, wq_half])
+    locals_[3].wait()
+    grad_z = wire.spread("col", lambda p: grad_cols.at[own], lambda p: grad_cols.at[own])
+    locals_[4].wait()
+    wo_half = halves(wo.shape[2])
+    wo_z = wire.spread(
+        "col", lambda p: wo.at[me_c, me_r, wo_half], lambda p: wo.at[me_c, me_r, wo_half]
+    )
+
+    for group in range(heads):
+        width = 3 * HD
+        bias_col[group * width : (group + 1) * width] = column_of(
+            bias_q[:, group * width : (group + 1) * width]
+        )
+    seg = seg_row[...].astype(wide)
+    for turn in range(cols):
+        here = slice(turn * block, (turn + 1) * block)
+        seg_col = column_of(seg[:, here])
+        up = lax.broadcasted_iota(jnp.int32, (block, count), 0) + turn * block
+        across = lax.broadcasted_iota(jnp.int32, (block, count), 1)
+        allowed = (across <= up) & (seg == seg_col)
+        mask[here] = jnp.where(allowed, 0.0, -jnp.inf)
+
+    for step in range(1, cols):
+        tok_z[step - 1].wait_recv()
+        there = rows_at(lax.rem(me_c + cols - step, cols), block)
+        tok_r.append(
+            wire.spread(
+                "row",
+                lambda p, there=there: tok.at[me_r, there],
+                lambda p, there=there: tok.at[me_r, there],
+            )
+        )
+    wq_s = []
+    for step in range(1, rows):
+        wq_r[step - 1].wait_recv()
+        peer = lax.rem(me_r + rows - step, rows)
+        wq_s.append(wire.push(wq.at[peer, wq_half], wq.at[peer, wq_half], "dp", 1 - me_d))
+    arrived(wo_z)
+    wo_r = wire.spread(
+        "row", lambda p: wo.at[:, me_r, wo_half], lambda p: wo.at[:, me_r, wo_half]
+    )
+    arrived(grad_z)
+    grad_r = wire.spread(
+        "row", lambda p: grad_cols.at[rows_at(p, block)], lambda p: grad_part.at[me_r]
+    )
+    locals_[5].wait()
+    wf_half = halves(feats)
+    wf_r = wire.spread("row", lambda p: wf.at[me_r, wf_half], lambda p: wf.at[me_r, wf_half])
+    locals_[6].wait()
+    wp_half = halves(wp.shape[1])
+    wp_r = wire.spread("row", lambda p: wp.at[me_r, wp_half], lambda p: wp.at[me_r, wp_half])
+    grad_part[me_r] = grad_cols[part]
+    for copies in tok_r:
+        arrived(copies)
+    arrived(vec_r)
+    arrived(wq_s)
+
+    def norm_block(turn, carry):
+        here = rows_at(turn, block)
+        values = [tok[slot, here, :].astype(wide) for slot in range(rows)]
+        mean = sum(jnp.sum(v, axis=1, keepdims=True) for v in values) / whole
+        square = sum(jnp.sum(v * v, axis=1, keepdims=True) for v in values) / whole
+        inv = lax.rsqrt(square - mean * mean + eps_norm)
+        mean_one[here] = mean
+        inv_one[here] = inv
+        total_ = bias_col[...]
+        for slot in range(rows):
+            unit = (values[slot] - mean) * inv
+            act = (unit * vecs[slot, 0:1, :] + vecs[slot, 1:2, :]).astype(low)
+            act_one[slot, here, :] = act
+            total_ = total_ + contract(wq[slot], act, 1, 1)
+        qkv[:, here] = total_.astype(low)
+        return carry
+
+    lax.fori_loop(0, cols, norm_block, 0)
+
+    def forward_head(head, carry):
+        base = head * 3 * HD
+        key = qkv[pl.ds(pl.multiple_of(base + HD, HD), HD), :]
+        value = qkv[pl.ds(pl.multiple_of(base + 2 * HD, HD), HD), :]
+        spot = rows_at(head, HD)
+        for turn in range(cols):
+            here = slice(turn * block, (turn + 1) * block)
+            reach = (turn + 1) * block
+            query = qkv[pl.ds(pl.multiple_of(base, HD), HD), here]
+            scores = contract(query, key[:, :reach], 0, 0) * score_scale + mask[here, :reach]
+            row_max = jnp.max(scores, axis=1, keepdims=True)
+            raised = jnp.exp(scores - row_max)
+            prob = raised * (1.0 / jnp.sum(raised, axis=1, keepdims=True))
+            probs[head, here, :reach] = prob
+            attn[spot, here] = contract(value[:, :reach], prob.astype(low), 1, 1).astype(low)
+        return carry
+
+    lax.fori_loop(0, heads, forward_head, 0)
+    attn_z = wire.spread(
+        "col", lambda p: attn.at[:, part], lambda p: attn_part.at[me_c]
+    )
+    attn_part[me_c] = attn[:, part]
+    arrived(wo_r)
+    wo_s = []
+    for step in range(1, rows):
+        peer = lax.rem(me_r + rows - step, rows)
+        wo_s.append(wire.push(wo.at[:, peer, wo_half], wo.at[:, peer, wo_half], "dp", 1 - me_d))
+    for step in range(1, cols):
+        peer = lax.rem(me_c + cols - step, cols)
+        wo_s.append(
+            wire.push(wo.at[peer, me_r, wo_half], wo.at[peer, me_r, wo_half], "dp", 1 - me_d)
+        )
+    wf_s, wp_s = [], []
+    for step in range(1, rows):
+        peer = lax.rem(me_r + rows - step, rows)
+        wf_r[step - 1].wait_recv()
+        wf_s.append(wire.push(wf.at[peer, wf_half], wf.at[peer, wf_half], "dp", 1 - me_d))
+    for step in range(1, rows):
+        peer = lax.rem(me_r + rows - step, rows)
+        wp_r[step - 1].wait_recv()
+        wp_s.append(wire.push(wp.at[peer, wp_half], wp.at[peer, wp_half], "dp", 1 - me_d))
+    arrived(wo_s)
+    arrived(grad_r)
+    arrived(attn_z)
+
+    turned = [attn_part[slot].T for slot in range(cols)]
+    mids = []
+    for slot in range(rows):
+        value = tok[slot, part, :].astype(wide) + vecs[slot, 4:5, :]
+        for across in range(cols):
+            value = value + contract(turned[across], wo[across, slot], 1, 0)
+        mid[slot] = value
+        mids.append(value)
+    mean = sum(jnp.sum(v, axis=1, keepdims=True) for v in mids) / whole
+    square = sum(jnp.sum(v * v, axis=1, keepdims=True) for v in mids) / whole
+    inv = lax.rsqrt(square - mean * mean + eps_norm)
+    inv_two[...] = inv
+    for slot in range(rows):
+        unit = (mids[slot] - mean) * inv
+        unit_two[slot] = unit
+        act_two[slot] = (unit * vecs[slot, 2:3, :] + vecs[slot, 3:4, :]).astype(low)
+    act_cols[part] = act_two[me_r]
+    arrived(wf_s)
+    arrived(wp_s)
+    pre = bias_f[...]
+    grad_hidden = None
+    for slot in range(rows):
+        pre = pre + contract(act_two[slot], wf[slot], 1, 0)
+        term = contract(grad_part[slot], wp[slot], 1, 1)
+        grad_hidden = term if grad_hidden is None else grad_hidden + term
+    curve = math.sqrt(2.0 / math.pi)
+    square = pre * pre
+    bend = jnp.tanh(curve * (pre + 0.044715 * (square * pre)))
+    hid[part] = (0.5 * pre * (1.0 + bend)).astype(low)
+    slope = 0.5 * (1.0 + bend) + 0.5 * pre * (1.0 - bend * bend) * (
+        curve * (1.0 + 3.0 * 0.044715 * square)
+    )
+    grad_pre = (slope * grad_hidden).astype(low)
+    gpre[part] = grad_pre
+    for slot in range(rows):
+        two_out[slot] = contract(grad_pre, wf[slot], 1, 1).astype(low)
+    two_z = wire.spread(
+        "col", lambda p: two_out.at[:, rows_at(p, piece)], lambda p: two_in.at[me_c]
+    )
+    hid_r = wire.spread("row", lambda p: hid.at[part], lambda p: hid.at[part])
+    gpre_r = wire.spread("row", lambda p: gpre.at[part], lambda p: gpre.at[part])
+    act_r = wire.spread("row", lambda p: act_two.at[p], lambda p: act_cols.at[part])
+    two_in[me_c] = two_out[:, bit, :]
+    arrived(two_z)
+
+    two_sums, scaled, units = [], [], []
+    for slot in range(rows):
+        value = two_in[0, slot].astype(wide)
+        for across in range(1, cols):
+            value = value + two_in[across, slot].astype(wide)
+        unit = unit_two[slot, bit, :]
+        two_sums.append(value)
+        units.append(unit)
+        scaled.append(value * vecs[slot, 2:3, :])
+        wide_out[slot] = jnp.concatenate(
+            [
+                jnp.sum(value * unit, axis=0, keepdims=True),
+                jnp.sum(value, axis=0, keepdims=True),
+            ],
+            axis=0,
+        )
+    first_mean = sum(jnp.sum(v, axis=1, keepdims=True) for v in scaled) / whole
+    second_mean = (
+        sum(jnp.sum(v * u, axis=1, keepdims=True) for v, u in zip(scaled, units)) / whole
+    )
+    inv_piece = inv_two[bit, :]
+    for slot in range(rows):
+        value = grad_part[slot, bit, :].astype(wide) + inv_piece * (
+            scaled[slot] - first_mean - units[slot] * second_mean
+        )
+        gm_piece[slot] = value.astype(low)
+    mid_z = wire.spread("col", lambda p: gm_piece, lambda p: mid_part.at[:, bit])
+    mid_part[:, bit, :] = gm_piece[...]
+    arrived(mid_z)
+
+    value = contract(wo[me_c, 0], mid_part[0], 1, 1)
+    for slot in range(1, rows):
+        value = value + contract(wo[me_c, slot], mid_part[slot], 1, 1)
+    gattn[:, part] = value.astype(low)
+    gattn_r = wire.spread("row", lambda p: gattn.at[:, part], lambda p: gattn.at[:, part])
+    mid_r = wire.spread("row", lambda p: mid_part.at[p], lambda p: mid_cols.at[part])
+    resid_r = wire.spread("row", lambda p: mid.at[p], lambda p: resid_own.at[part])
+    mid_cols[part] = mid_part[me_r]
+    resid_own[part] = mid[me_r]
+
+    arrived(hid_r)
+    arrived(gpre_r)
+    arrived(act_r)
+    sum_f[me_d] = contract(act_cols[...], gpre[...], 0, 0).astype(low)
+    pair = [wire.push(sum_f.at[me_d], sum_f.at[me_d], "dp", 1 - me_d)]
+    sum_p[me_d] = contract(hid[...], grad_cols[...], 0, 0).astype(low)
+    pair.append(wire.push(sum_p.at[me_d], sum_p.at[me_d], "dp", 1 - me_d))
+    ones = jnp.ones((8, count), low)
+    sum_bf[me_d] = contract(ones, gpre[...], 1, 0)
+    pair.append(wire.push(sum_bf.at[me_d], sum_bf.at[me_d], "dp", 1 - me_d))
+    outward[...] = contract(hid[...], wp[me_r], 1, 0).astype(low)
+    arrived(gattn_r)
+
+    def backward_head(head, carry):
+        base = head * 3 * HD
+        spot_q = pl.ds(pl.multiple_of(base, HD), HD)
+        spot_k = pl.ds(pl.multiple_of(base + HD, HD), HD)
+        spot_v = pl.ds(pl.multiple_of(base + 2 * HD, HD), HD)
+        spot = rows_at(head, HD)
+        key, value = qkv[spot_k, :], qkv[spot_v, :]
+        for turn in reversed(range(cols)):
+            here = slice(turn * block, (turn + 1) * block)
+            reach = (turn + 1) * block
+            query = qkv[spot_q, here]
+            grads = gattn[spot, here]
+            dots = grads.astype(wide) * attn[spot, here].astype(wide)
+            row_dot = jnp.sum(dots.T, axis=1, keepdims=True)
+            prob = probs[head, here, :reach]
+            grad_probs = contract(grads, value[:, :reach], 0, 0)
+            grad_scores = (score_scale * prob * (grad_probs - row_dot)).astype(low)
+            gqkv[spot_q, here] = contract(key[:, :reach], grad_scores, 1, 1).astype(low)
+            term_k = contract(query, grad_scores, 1, 0)
+            term_v = contract(grads, prob.astype(low), 1, 0)
+            if turn == cols - 1:
+                acc_k[...] = term_k
+                acc_v[...] = term_v
+            else:
+                acc_k[:, :reach] += term_k
+                acc_v[:, :reach] += term_v
+        gqkv[spot_k, :] = acc_k[...].astype(low)
+        gqkv[spot_v, :] = acc_v[...].astype(low)
+        return carry
+
+    lax.fori_loop(0, heads, backward_head, 0)
+    sum_q[me_d] = contract(act_one[me_r], gqkv[...], 0, 1).astype(low)
+    pair.append(wire.push(sum_q.at[me_d], sum_q.at[me_d], "dp", 1 - me_d))
+    sum_bq[me_d] = contract(ones, gqkv[...], 1, 1)
+    pair.append(wire.push(sum_bq.at[me_d], sum_bq.at[me_d], "dp", 1 - me_d))
+    arrived(mid_r)
+    sum_o[me_d] = contract(attn[...], mid_cols[...], 1, 0).astype(low)
+    pair.append(wire.push(sum_o.at[me_d], sum_o.at[me_d], "dp", 1 - me_d))
+    inward[...] = contract(gqkv[...], wq[me_r], 0, 0).astype(low)
+    mid_own[...] = mid_cols[own]
+    inv = inv_one[own]
+    inv_own[...] = inv
+    unit_own[...] = (tok[me_r, own].astype(wide) - mean_one[own]) * inv
+    arrived(resid_r)
+    arrived(pair)
+    wire.drain()
+
+
+def front(tokens, out_grad, segment_ids, w_qkv, w_out, w_fc, w_proj, bias_qkv, bias_fc, row_vectors):
+    low, wide = jnp.bfloat16, jnp.float32
+    rows, cols = lax.axis_size("row"), lax.axis_size("col")
+    block, feats = tokens.shape
+    count = block * cols
+    piece = block // cols
+    width, hidden = w_qkv.shape[1], w_fc.shape[1]
+    heads = width // (3 * HD)
+    shape = jax.ShapeDtypeStruct
+    outs = [
+        shape((2, feats, width), low),
+        shape((2, w_out.shape[0], feats), low),
+        shape((2, feats, hidden), low),
+        shape((2, hidden, feats), low),
+        shape((2, 8, width), wide),
+        shape((2, 8, hidden), wide),
+        shape((count, feats), low),
+        shape((count, feats), low),
+        shape((block, feats), wide),
+        shape((block, 1), wide),
+        shape((block, feats), low),
+        shape((count, feats), wide),
+        shape((rows, 2, feats), wide),
+    ]
+    buffers = [
+        ((rows, count, feats), low),
+        ((count, feats), low),
+        ((rows, block, feats), low),
+        ((rows, row_vectors.shape[0], feats), wide),
+        ((rows, width, feats), low),
+        ((cols, rows, w_out.shape[0], feats), low),
+        ((rows, feats, hidden), low),
+        ((rows, hidden, feats), low),
+        ((rows, count, feats), low),
+        ((width, count), low),
+        ((width, 1), wide),
+        ((count, count), wide),
+        ((heads, count, count), wide),
+        ((heads * HD, count), low),
+        ((cols, heads * HD, block), low),
+        ((rows, block, feats), wide),
+        ((block, 1), wide),
+        ((rows, block, feats), low),
+        ((count, feats), low),
+        ((rows, block, feats), wide),
+        ((count, hidden), low),
+        ((count, hidden), low),
+        ((rows, block, feats), low),
+        ((cols, rows, piece, feats), low),
+        ((rows, piece, feats), low),
+        ((rows, block, feats), low),
+        ((count, feats), low),
+        ((heads * HD, count), low),
+        ((width, count), low),
+        ((HD, count), wide),
+        ((HD, count), wide),
+        ((count, 1), wide),
+        ((count, 1), wide),
+    ]
+    loose = pl.BlockSpec(memory_space=pl.ANY)
+    near = pl.BlockSpec(memory_space=pltpu.VMEM)
+    return pl.pallas_call(
+        front_kernel,
+        out_shape=outs,
+        in_specs=[loose, loose, near, loose, loose, loose, loose, near, near, loose],
+        out_specs=[near] * len(outs),
+        scratch_shapes=[pltpu.VMEM(size, kind) for size, kind in buffers]
+        + [
+            pltpu.SemaphoreType.DMA((front_wires,)),
+            pltpu.SemaphoreType.DMA((front_wires,)),
+            pltpu.SemaphoreType.DMA((7,)),
+        ],
+        compiler_params=pltpu.CompilerParams(collective_id=20, has_side_effects=True),
+    )(
+        tokens,
+        out_grad,
+        segment_ids,
+        w_qkv.T,
+        w_out,
+        w_fc,
+        w_proj,
+        bias_qkv[None],
+        bias_fc[None],
+        row_vectors,
+    )
+
+
 def local(
     tokens,
     out_grad,
@@ -539,6 +1021,223 @@
     )
 
 
+def paired_local(
+    tokens,
+    out_grad,
+    segment_ids,
+    w_qkv,
+    w_out,
+    w_fc,
+    w_proj,
+    bias_qkv,
+    bias_fc,
+    row_vectors,
+    mom_qkv,
+    mom_out,
+    mom_fc,
+    mom_proj,
+    mom_bias_qkv,
+    mom_bias_fc,
+    mom_rows,
+):
+    low = jnp.bfloat16
+    score_scale = 1.0 / math.sqrt(HD)
+    row_parts = lax.axis_size("row")
+    col_parts = lax.axis_size("col")
+    dp_parts = lax.axis_size("dp")
+    own_tokens, own_features = tokens.shape
+    token_count = own_tokens * col_parts
+    feature_count = own_features * row_parts
+    token_base = lax.axis_index("col") * own_tokens
+    feature_base = lax.axis_index("row") * own_features
+
+    def own_columns(whole):
+        return lax.dynamic_slice_in_dim(whole, feature_base, own_features, 1)
+
+    def own_block(whole):
+        return lax.dynamic_slice(whole, (token_base, feature_base), (own_tokens, own_features))
+
+    def own_rows(whole):
+        return lax.dynamic_slice_in_dim(whole, token_base, own_tokens, 0)
+
+    proj_flip = w_proj.T
+    (
+        slots_q, slots_o, slots_f, slots_p, slots_bq, slots_bf, outward, inward, unit_one_own,
+        inv_own, mid_own, resid_all, wide_terms,
+    ) = front(
+        tokens, out_grad, segment_ids, w_qkv, w_out, w_fc, w_proj, bias_qkv, bias_fc, row_vectors
+    )
+    resid_own = own_rows(resid_all)
+    summed = [total(slots) for slots in (slots_q, slots_o, slots_f, slots_p)]
+    summed = summed + [total(slots_bq)[0], total(slots_bf)[0]]
+
+    weights = (w_qkv, w_out, w_fc, w_proj)
+    moments = (mom_qkv, mom_out, mom_fc, mom_proj)
+    flips = (False, True, False, True)
+    new_moms = [beta_mom * moments[member] + summed[member] for member in range(4)]
+    pushes = [
+        (summed[member] + beta_mom * new_moms[member]).astype(low) for member in range(4)
+    ]
+    upright = [pushes[member].T if flips[member] else pushes[member] for member in range(4)]
+    widest = max(piece.shape[1] for piece in upright)
+    share = -(-widest // dp_parts)
+    assert row_parts == len(upright)
+    outgoing = jnp.stack(
+        [
+            jnp.pad(piece, ((0, 0), (0, share * dp_parts - piece.shape[1])))
+            for piece in upright
+        ]
+    )
+    outgoing = lax.dynamic_slice_in_dim(outgoing, lax.axis_index("dp") * share, share, 2)
+    arrived, block_slots, one_slots = exchange(
+        ["row", "col", "col"],
+        [
+            outgoing,
+            outward.reshape(col_parts, own_tokens, own_features),
+            inward.reshape(col_parts, own_tokens, own_features),
+        ],
+        [True] * 3,
+        7,
+    )
+    matrix = arrived.reshape(feature_count, share)
+    gram_low = product(matrix, matrix, True).astype(low)
+    edge = feature_count // 3
+    spots = [(0, 0), (0, 1), (0, 2), (1, 1), (1, 2), (2, 2)]
+    packed = jnp.concatenate(
+        [
+            gram_low[up * edge : (up + 1) * edge, across * edge : (across + 1) * edge]
+            for up, across in spots
+        ],
+        axis=0,
+    )
+    block_out = (resid_own + total(block_slots) + row_vectors[5]).astype(low)
+    grad_norm_one = total(one_slots)
+    scaled_one = grad_norm_one * row_vectors[0]
+    stat_pair = jnp.stack(
+        [jnp.sum(scaled_one, axis=1), jnp.sum(scaled_one * unit_one_own, axis=1)]
+    )
+    wide_slot_terms = wide_terms
+    if dp_parts == 2:
+        stat_slots, wide_slots, half_slots = exchange(
+            ["row", "row", "dp"],
+            [stat_pair, wide_slot_terms, packed.reshape(dp_parts, -1, edge)],
+            [False, True, True],
+            8,
+        )
+        gram_half = total(half_slots).astype(low)
+    else:
+        stat_slots, wide_slots = exchange(
+            "row", [stat_pair, wide_slot_terms], [False, True], 8
+        )
+        gram_half = lax.psum(packed, "dp")
+    stat_sum = total(stat_slots)
+    first_sum, second_sum = stat_sum[0][:, None], stat_sum[1][:, None]
+    wide_sum = total(wide_slots)
+    input_grad = mid_own.astype(jnp.float32) + inv_own * (
+        scaled_one - first_sum / feature_count - unit_one_own * (second_sum / feature_count)
+    )
+    row_terms = jnp.stack(
+        [
+            jnp.sum(grad_norm_one * unit_one_own, axis=0),
+            jnp.sum(grad_norm_one, axis=0),
+            wide_sum[0],
+            wide_sum[1],
+            jnp.sum(mid_own, axis=0, dtype=jnp.float32),
+            jnp.sum(out_grad, axis=0, dtype=jnp.float32),
+        ]
+    )
+    quarter_slots, term_slots = exchange(
+        "col",
+        [gram_half.reshape(col_parts, -1, edge), row_terms],
+        [True, False],
+        9,
+    )
+    (whole_slots,) = exchange("col", [total(quarter_slots).astype(low)], [False], 10)
+    gram_half = whole_slots.reshape(gram_half.shape)
+    if dp_parts == 2:
+        gram_slots, pair_slots = exchange(
+            "dp", [gram_half, total(term_slots)], [False, False], 11
+        )
+        gram_half = gram_slots
+    else:
+        (pair_slots,) = exchange("dp", [total(term_slots)], [False], 11)
+    grad_rows = total(pair_slots)
+    tiles = gram_half.reshape(len(spots), edge, edge)
+    found = {spot: tiles[which] for which, spot in enumerate(spots)}
+    gram = jnp.concatenate(
+        [
+            jnp.concatenate(
+                [
+                    found[up, across] if across >= up else found[across, up].T
+                    for across in range(3)
+                ],
+                axis=1,
+            )
+            for up in range(3)
+        ],
+        axis=0,
+    ).astype(jnp.float32)
+    factor, scale, gram_norm = polynomial_factor(gram)
+    ortho = (scale * matrix.astype(jnp.float32) + matrix_product(factor, matrix)) * lax.rsqrt(
+        gram_norm
+    )
+    (back,) = exchange(
+        "row", [ortho.astype(low).reshape(row_parts, own_features, share)], [True], 12
+    )
+    if dp_parts == 2:
+        (ortho_slots,) = exchange("dp", [back], [False], 13)
+        orthos = jnp.concatenate([ortho_slots[part] for part in range(dp_parts)], axis=2)
+    else:
+        orthos = lax.all_gather(back, "dp", axis=2, tiled=True)
+    new_weights = []
+    for member in range(4):
+        piece = orthos[member, :, : upright[member].shape[1]]
+        if flips[member]:
+            piece = piece.T
+        longest = max(
+            upright[member].shape[0] * row_parts, upright[member].shape[1] * col_parts
+        )
+        new_weights.append(
+            weights[member].astype(jnp.float32)
+            - rate_matrix * math.sqrt(longest) * piece.astype(jnp.float32)
+        )
+
+    vector_rate = rate_vector / math.sqrt(token_count * dp_parts)
+
+    def vector_step(weight, gradient, moment):
+        new_moment = beta_mom * moment + gradient
+        return (weight - vector_rate * (gradient + beta_mom * new_moment), new_moment)
+
+    new_bias_qkv, new_mom_bias_qkv = vector_step(bias_qkv, summed[4], mom_bias_qkv)
+    new_bias_fc, new_mom_bias_fc = vector_step(bias_fc, summed[5], mom_bias_fc)
+    new_rows, new_mom_rows = vector_step(row_vectors, grad_rows, mom_rows)
+    return (
+        block_out,
+        input_grad,
+        summed[0],
+        summed[1],
+        summed[2],
+        summed[3],
+        summed[4],
+        summed[5],
+        grad_rows,
+        new_weights[0],
+        new_weights[1],
+        new_weights[2],
+        new_weights[3],
+        new_bias_qkv,
+        new_bias_fc,
+        new_rows,
+        new_moms[0],
+        new_moms[1],
+        new_moms[2],
+        new_moms[3],
+        new_mom_bias_qkv,
+        new_mom_bias_fc,
+        new_mom_rows,
+    )
+
+
 def solution(mesh):
     placed = (
         P(("dp", "col"), "row"),
@@ -560,7 +1259,7 @@
         P(None, "row"),
     )
     return jax.shard_map(
-        local,
+        paired_local if mesh.shape["dp"] == 2 else local,
         mesh=mesh,
         in_specs=placed,
         out_specs=(

time: 353 us -> 217 us (0.61)
  Pallas kernels: 215 us -> 157 us
  local copies, waits for them, and re-layouts: 48.9 us -> 20 us
  matrix products: 37 us -> 13 us
  other arithmetic: 44.6 us -> 22.5 us
    pallas_call x15 -> x7, Pallas kernels: 215 us -> 69 us  [exchange(): pl.pallas_call(functools.partial(exchange_kernel, tuple(axes), tuple(part...]
    pallas_call x0 -> x1, Pallas kernels: none -> 87.7 us  [front(): pl.pallas_call(front_kernel, out_shape=outs, in_specs=[loose, loose, near...]
    dot_general x13 -> x0, matrix products: 16.1 us -> none  [the longest x4 6.71 us: inner_rows(): lax.dot_general(left_side, right_side, (((0,), (0,)), ((), ())), preferre...]
    convert_element_type x6 -> x1, other arithmetic: 9.15 us -> 0.86 us  [paired_local(): (summed[member] + beta_mom * new_moms[member]).astype(low)]
    reduce_sum x10 -> x4, other arithmetic: 8.78 us -> 2.33 us  [the longest x1 1.07 us: paired_local(): jnp.sum(grad_norm_one, axis=0)]
    unnamed x126 -> x85, local copies, waits for them, and re-layouts: 18 us -> 12.3 us
    convert_element_type x5 -> x0, local copies, waits for them, and re-layouts: 5.09 us -> none  [the longest x1 1.74 us: local(): act_two = (unit_two * gain_two + shift_two).astype(low)]
    reshape x4 -> x0, local copies, waits for them, and re-layouts: 3.88 us -> none  [the longest x2 3.76 us: local(): rows.reshape(part_tokens, row_parts, own_features).transpose(1, 0, 2)]
where the time goes in v1:
time: 217 us; the launch traced here: 214 us
  Pallas kernels  157 us (72%)
  other arithmetic  22.5 us (10%)
  local copies, waits for them, and re-layouts  20 us (9%)
  matrix products  13 us (6%)
    pallas_call x1, Pallas kernels, front(): pl.pallas_call(front_kernel, out_shape=outs, in_specs=[loose, loose, near...  87.7 us
    pallas_call x7, Pallas kernels, exchange(): pl.pallas_call(functools.partial(exchange_kernel, tuple(axes), tuple(part...  69 us
    unnamed x85, local copies, waits for them, and re-layouts  12.3 us
    dot_general x5, matrix products, matrix_product(): jnp.dot(left_side.astype(jnp.bfloat16), right_side.astype(jnp.bfloat16),...  10.9 us
    reduce_sum x13, other arithmetic, total(): return jnp.sum(slots.astype(jnp.float32), axis=0)  8.14 us

profile of v1, /device:TPU:25, one launch (start us, length us, event | category | flops | bytes accessed | tf_op | source)
XLA Modules:
  0.0 214.2 jit_solution(2277116045279018491)
XLA Ops:
  0.7 1.6 copy.73.refs_0_
  2.3 1.5 copy.74.refs_1_
  3.8 1.8 copy.72
  5.6 1.9 copy.75.refs_6_
  7.5 1.3 broadcast_in_dim.6.refs_7_
  8.7 1.3 broadcast_in_dim.7.refs_8_
  10.0 87.7 %shard_map.344 = (bf16[2,192,576]{2,1,0:T(8,128)(2,1)}, bf16[2,192,192]{2,1,0:T(8,128)(2,1)}, bf16[2,192,768]{2,1,0:T(8,128)(2,1)}, bf16[2,768,192]{2,1,0:T(8,12...) custom-call(bf16[128,192]{1,0:T(8,128)(2,1)} %copy.73.refs_0_, ...), custom_call_target="tpu_custom_call" | custom-call | tf_op jit(solution)/shard_map/pallas_call | solution.py:612
  97.7 1.2 convert_reduce_fusion.2
  101.8 1.0 fusion.15
  103.2 2.2 %fusion.16 = (bf16[1,192,768]{2,1,0:T(8,128)(2,1)S(1)}, f32[768,192]{0,1:T(8,128)}) fusion(f32[768,192]{0,1:T(8,128)S(1)} %copy.80, f32[768,192]{0,1:T(8,128)} %param.30), kind=kLoop, calls=%fused_computation.45 | loop fusion | flops 737280 | bytes 2064384 | tf_op jit(solution)/shard_map/stack | solution.py:1085
  106.3 16.1 %shard_map.345 = (bf16[4,192,384]{2,1,0:T(8,128)(2,1)}, bf16[4,128,192]{2,1,0:T(8,128)(2,1)}, bf16[4,128,192]{2,1,0:T(8,128)(2,1)}) custom-call(bf16[4,192,384]{2,1,0:T(8,128)(2,1)} %fusion.14.refs_0_, bf16[4,128,192]{2,1,0:T(8,128)(2,1)} %bitcast.85, bf16[4,128,192]{2,1,0:T(8,128)(2,1)} %bitcast.86), custom_call_target="tpu_custom_call" | custom-call | tf_op jit(solution)/shard_map/pallas_call | solution.py:100
  122.4 1.1 convert_reduce_fusion.3
  124.2 2.1 convolution_convert_fusion
  126.4 0.9 copy-done.6
  127.3 6.5 %shard_map.346 = (f32[4,2,128]{2,1,0:T(2,128)}, f32[4,2,192]{2,1,0:T(2,128)}, bf16[2,768,256]{2,1,0:T(8,128)(2,1)}) custom-call(f32[2,128]{1,0:T(2,128)} %pad_maximum_fusion.2.refs_0_, f32[4,2,192]{2,1,0:T(2,128)} %get-tuple-element.58.refs_1_, bf16[2,768,256]{2,1,0:T(8,128)(2,1)} %bitcast.81), custom_call_target="tpu_custom_call" | custom-call | tf_op jit(solution)/shard_map/pallas_call | solution.py:100
  134.7 1.0 convert_reduce_fusion.7
  138.5 2.1 reduce_sum.206
  141.3 10.7 %shard_map.347 = (bf16[4,192,256]{2,1,0:T(8,128)(2,1)}, f32[4,6,192]{2,1,0:T(8,128)}) custom-call(bf16[4,192,256]{2,1,0:T(8,128)(2,1)} %bitcast.70, f32[6,192]{1,0:T(8,128)} %stack.51.refs_1_), custom_call_target="tpu_custom_call" | custom-call | tf_op jit(solution)/shard_map/pallas_call | solution.py:100
  152.1 1.7 reduce_sum.212.refs_0_
  153.8 11.5 %shard_map.348 = bf16[4,192,256]{2,1,0:T(8,128)(2,1)} custom-call(bf16[192,256]{1,0:T(8,128)(2,1)} %reduce_sum.212.refs_0_), custom_call_target="tpu_custom_call" | custom-call | tf_op jit(solution)/shard_map/pallas_call | solution.py:100
  165.3 1.4 reduce_sum.213.refs_1_
  166.6 7.7 %shard_map.349 = (bf16[2,768,256]{2,1,0:T(8,128)(2,1)}, f32[2,6,192]{2,1,0:T(8,128)}) custom-call(bf16[768,256]{1,0:T(8,128)(2,1)} %bitcast.71, f32[6,192]{1,0:T(8,128)} %reduce_sum.213.refs_1_), custom_call_target="tpu_custom_call" | custom-call | tf_op jit(solution)/shard_map/pallas_call | solution.py:100
  175.1 1.3 fusion.23
  177.0 1.2 fusion
  178.9 1.2 multiply_add_fusion.4
  180.1 1.1 multiply_add_fusion.3
  181.2 1.1 multiply_add_fusion.2
  182.4 2.5 %multiply_add_fusion.1 = f32[768,768]{1,0:T(8,128)} fusion(f32[768,768]{1,0:T(8,128)S(1)} %multiply_add_fusion.2), kind=kOutput, calls=%fused_computation.5 | convolution fusion | flops 908328960 | bytes 4718592 | tf_op jit(solution)/shard_map/dot_general | solution.py:130
  185.0 4.9 %fusion.3 = bf16[768,384]{1,0:T(8,128)(2,1)} fusion(bf16[768,384]{1,0:T(8,128)(2,1)S(1)} %bitcast.69, f32[768,768]{1,0:T(8,128)S(1)} %multiply_add_fusion.4, f32[768,768]{1,0:T(8,128)} %multiply_add_fusion.1, f32[]{:T(128)S(6)} %rsqrt.3), kind=kOutput, calls=%fused_computation.13 | convolution fusion | flops 1363968000 | bytes 5898244 | tf_op jit(solution)/shard_map/dot_general | solution.py:130
  189.9 12.3 %shard_map.350.refs_0_ = bf16[4,192,384]{2,1,0:T(8,128)(2,1)} custom-call(bf16[4,192,384]{2,1,0:T(8,128)(2,1)} %bitcast.83), custom_call_target="tpu_custom_call" | custom-call | tf_op jit(solution)/shard_map/pallas_call | solution.py:100
  202.2 4.3 %shard_map.351 = bf16[2,4,192,384]{3,2,1,0:T(8,128)(2,1)} custom-call(bf16[4,192,384]{2,1,0:T(8,128)(2,1)} %shard_map.350.refs_0_), custom_call_target="tpu_custom_call" | custom-call | tf_op jit(solution)/shard_map/pallas_call | solution.py:100
  206.5 1.4 slice_bitcast_fusion.1
  (116 shorter events, 16.7 us)
Async XLA Ops:
  0.7 99.0 %copy-start.14 = (f32[192,576]{1,0:T(8,128)S(1)}, f32[192,576]{1,0:T(8,128)}, u32[]{:S(2)}) copy-start(f32[192,576]{1,0:T(8,128)} %param.27) | copy-start | bytes 1327108
  10.0 90.8 %copy-start.18 = (f32[192,192]{1,0:T(8,128)S(1)}, f32[192,192]{1,0:T(8,128)}, u32[]{:S(2)}) copy-start(f32[192,192]{1,0:T(8,128)} %param.28) | copy-start | bytes 442372
  97.7 2.9 %copy-start.19 = (bf16[2,192,192]{2,1,0:T(8,128)(2,1)S(1)}, bf16[2,192,192]{2,1,0:T(8,128)(2,1)}, u32[]{:S(2)}) copy-start(bf16[2,192,192]{2,1,0:T(8,128)(2,1)} %get-tuple-element.48) | copy-start | bytes 442372
  99.7 2.0 copy-start.11
  100.6 1.2 copy-start.12
  100.6 2.1 copy-start.9
  100.9 1.9 copy-start.8
  101.8 1.4 copy-start.1
  103.2 19.2 %copy-start.2 = (f32[768,192]{0,1:T(8,128)}, f32[768,192]{0,1:T(8,128)S(1)}, u32[]{:S(2)}) copy-start(f32[768,192]{0,1:T(8,128)S(1)} %copy.80) | copy-start | bytes 1769476
  103.2 20.3 %copy-start.23 = (f32[6,192]{1,0:T(8,128)S(1)}, f32[6,192]{1,0:T(8,128)}, u32[]{:S(2)}) copy-start(f32[6,192]{1,0:T(8,128)} %refs_9_.1) | copy-start | bytes 13828
  103.2 20.3 %copy-start.13 = (f32[128,192]{1,0:T(8,128)S(1)}, f32[128,192]{1,0:T(8,128)}, u32[]{:S(2)}) copy-start(f32[128,192]{1,0:T(8,128)} %get-tuple-element.57) | copy-start | bytes 294916
  124.2 10.4 %copy-start.21 = (f32[128,1]{1,0:T(8,128)S(1)}, f32[128,1]{1,0:T(8,128)}, u32[]{:S(2)}) copy-start(f32[128,1]{1,0:T(8,128)} %get-tuple-element.55) | copy-start | bytes 1540
  124.2 10.5 %copy-start.16 = (bf16[4,128,192]{2,1,0:T(8,128)(2,1)S(1)}, bf16[4,128,192]{2,1,0:T(8,128)(2,1)}, u32[]{:S(2)}) copy-start(bf16[4,128,192]{2,1,0:T(8,128)(2,1)} %get-tuple-element.53) | copy-start | bytes 589828
  124.2 10.5 %copy-start.20 = (bf16[128,192]{1,0:T(8,128)(2,1)S(1)}, bf16[128,192]{1,0:T(8,128)(2,1)}, u32[]{:S(2)}) copy-start(bf16[128,192]{1,0:T(8,128)(2,1)} %get-tuple-element.54) | copy-start | bytes 147460
  126.3 10.9 %copy-start.24 = (f32[2,8,576]{2,1,0:T(8,128)S(1)}, f32[2,8,576]{2,1,0:T(8,128)}, u32[]{:S(2)}) copy-start(f32[2,8,576]{2,1,0:T(8,128)} %get-tuple-element.61) | copy-start | bytes 110596
  126.3 11.6 %copy-start.22 = (f32[2,8,768]{2,1,0:T(8,128)S(1)}, f32[2,8,768]{2,1,0:T(8,128)}, u32[]{:S(2)}) copy-start(f32[2,8,768]{2,1,0:T(8,128)} %get-tuple-element.62) | copy-start | bytes 147460
  126.4 14.3 %copy-start.17 = (bf16[128,192]{0,1:T(8,128)(2,1)S(1)}, bf16[128,192]{0,1:T(8,128)(2,1)}, u32[]{:S(2)}) copy-start(bf16[128,192]{0,1:T(8,128)(2,1)} %param.18) | copy-start | bytes 147460
  133.8 6.7 %copy-start.31 = (f32[4,2,192]{2,1,0:T(2,128)S(1)}, f32[4,2,192]{2,1,0:T(2,128)}, u32[]{:S(2)}) copy-start(f32[4,2,192]{2,1,0:T(2,128)} %get-tuple-element.64) | copy-start | bytes 18436
  175.1 37.7 %copy-start.25 = (f32[6,192]{1,0:T(8,128)}, f32[6,192]{1,0:T(8,128)S(1)}, u32[]{:S(2)}) copy-start(f32[6,192]{1,0:T(8,128)S(1)} %reduce_sum.214) | copy-start | bytes 13828
  182.4 2.6 %copy-start = (bf16[4,192,384]{2,1,0:T(8,128)(2,1)S(1)}, bf16[4,192,384]{2,1,0:T(8,128)(2,1)}, u32[]{:S(2)}) copy-start(bf16[4,192,384]{2,1,0:T(8,128)(2,1)} %get-tuple-element.59) | copy-start | bytes 1769476
  202.2 5.7 %copy-start.7 = (bf16[192,576]{1,0:T(8,128)(2,1)S(1)}, bf16[192,576]{1,0:T(8,128)(2,1)}, u32[]{:S(2)}) copy-start(bf16[192,576]{1,0:T(8,128)(2,1)} %param.20) | copy-start | bytes 663556
  206.4 2.3 %copy-start.15 = (bf16[192,192]{1,0:T(8,128)(2,1)S(1)}, bf16[192,192]{1,0:T(8,128)(2,1)}, u32[]{:S(2)}) copy-start(bf16[192,192]{1,0:T(8,128)(2,1)} %refs_4_.1) | copy-start | bytes 221188
  206.5 3.3 %copy-start.4 = (bf16[192,768]{1,0:T(8,128)(2,1)S(1)}, bf16[192,768]{1,0:T(8,128)(2,1)}, u32[]{:S(2)}) copy-start(bf16[192,768]{1,0:T(8,128)(2,1)} %refs_5_.1) | copy-start | bytes 884740
  207.9 2.8 %copy-start.5 = (bf16[768,192]{0,1:T(8,128)(2,1)S(1)}, bf16[768,192]{0,1:T(8,128)(2,1)}, u32[]{:S(2)}) copy-start(bf16[768,192]{0,1:T(8,128)(2,1)} %param.23) | copy-start | bytes 884740
  208.9 2.7 %copy-start.28 = (f32[576]{0:T(1024)S(1)}, f32[576]{0:T(1024)}, u32[]{:S(2)}) copy-start(f32[576]{0:T(1024)} %param.24) | copy-start | bytes 6916
  208.9 2.7 %copy-start.29 = (f32[576]{0:T(1024)S(1)}, f32[576]{0:T(1024)}, u32[]{:S(2)}) copy-start(f32[576]{0:T(1024)} %slice_reduce_fusion.1) | copy-start | bytes 6916
  208.9 2.7 %copy-start.32 = (f32[576]{0:T(1024)S(1)}, f32[576]{0:T(1024)}, u32[]{:S(2)}) copy-start(f32[576]{0:T(1024)} %param.31) | copy-start | bytes 6916
  208.9 3.3 %copy-start.26 = (f32[768]{0:T(1024)S(1)}, f32[768]{0:T(1024)}, u32[]{:S(2)}) copy-start(f32[768]{0:T(1024)} %param.25) | copy-start | bytes 9220
  209.0 3.3 %copy-start.27 = (f32[768]{0:T(1024)S(1)}, f32[768]{0:T(1024)}, u32[]{:S(2)}) copy-start(f32[768]{0:T(1024)} %slice_reduce_fusion) | copy-start | bytes 9220
  209.0 3.2 %copy-start.33 = (f32[768]{0:T(1024)S(1)}, f32[768]{0:T(1024)}, u32[]{:S(2)}) copy-start(f32[768]{0:T(1024)} %param.32) | copy-start | bytes 9220
  209.0 3.8 %copy-start.30 = (f32[6,192]{1,0:T(8,128)S(1)}, f32[6,192]{1,0:T(8,128)}, u32[]{:S(2)}) copy-start(f32[6,192]{1,0:T(8,128)} %param.33) | copy-start | bytes 13828
  209.0 4.4 %copy-start.10 = (f32[192,192]{0,1:T(8,128)S(1)}, f32[192,192]{0,1:T(8,128)}, u32[]{:S(2)}) copy-start(f32[192,192]{0,1:T(8,128)} %get-tuple-element.164) | copy-start | bytes 442372
  (2 other events, 1.7 us)

commit v2 on v1

--- a/solution.py
+++ b/solution.py
@@ -214,7 +214,7 @@
                 barrier, inc=1, device_id={axis: peer}, device_id_type=pl.DeviceIdType.MESH
             )
             met += 1
-    pl.semaphore_wait(barrier, met)
+    return lambda: pl.semaphore_wait(barrier, met)
 
 
 def arrived(copies):
@@ -226,74 +226,83 @@
     return pl.ds(pl.multiple_of(index * size, size), size)
 
 
-front_wires = 110
-
-
-def front_kernel(*refs):
+step_wires = 180
+
+
+def step_kernel(*refs):
     low, wide = jnp.bfloat16, jnp.float32
     (
         tok_in, grad_in, seg_row, wq_in, wo_in, wf_in, wp_in, bias_q, bias_f, vec_in,
-        sum_q, sum_o, sum_f, sum_p, sum_bq, sum_bf, outward, inward, unit_own, inv_own,
-        mid_own, resid_own, wide_out,
-        tok, grad_cols, grad_part, vecs, wq, wo, wf, wp, act_one, qkv, bias_col, mask, probs,
-        attn, attn_part, unit_two, inv_two, act_two, act_cols, mid, hid, gpre, two_out, two_in,
-        gm_piece, mid_part, mid_cols, gattn, gqkv, acc_k, acc_v, mean_one, inv_one,
+        mom_q_in, mom_o_in, mom_f_in, mom_p_in,
+        sum_q, sum_o, sum_f, sum_p, sum_bq, sum_bf, block_out, input_grad, grad_rows, back,
+        tok, grad_cols, grad_turn, grad_part, vecs, wq_own, wq, wo, wf, wp, act_one, qkv,
+        bias_col, gains, mask, probs,
+        attn, attn_part, unit_two, inv_two, act_two, act_cols, mid, resid, hid, gpre, two_out,
+        two_in, gm_piece, mid_part, mid_cols, gattn, gqkv, acc_k, acc_v, mean_one, inv_one,
+        wide_out, wide_in, outward, outward_in, inward, inward_in, stat_out, stat_in,
+        term_out, term_in, term_pair, mom_q, mom_o, mom_f, mom_p, pushed, matrix, packed,
+        packed_in, halved, quarter_in, gathered, gram, ortho,
         send_sem, recv_sem, local_sem,
     ) = refs
     rows, cols = lax.axis_size("row"), lax.axis_size("col")
     me_r, me_c, me_d = lax.axis_index("row"), lax.axis_index("col"), lax.axis_index("dp")
-    count, feats = tok.shape[1], tok.shape[2]
+    other = 1 - me_d
+    feats, count = tok.shape[1], tok.shape[2]
     whole = feats * rows
     block = count // cols
     piece = block // cols
-    half = feats // 2
     heads = qkv.shape[0] // (3 * HD)
     score_scale = 1.0 / math.sqrt(HD)
     own = rows_at(me_c, block)
     part = rows_at(me_r, block)
     bit = rows_at(me_c, piece)
     wire = Wire(send_sem, recv_sem)
+    met = greet(("row", "col", "dp"))
     locals_ = []
     for which, (source, target) in enumerate(
         [
-            (tok_in, tok.at[me_r, own]),
+            (tok_in, tok.at[me_r, :, own]),
             (vec_in, vecs.at[me_r]),
-            (wq_in, wq.at[me_r]),
-            (grad_in, grad_cols.at[own]),
+            (wq_in, wq_own),
+            (grad_in, grad_cols.at[:, own]),
             (wo_in, wo.at[me_c, me_r]),
             (wf_in, wf.at[me_r]),
             (wp_in, wp.at[me_r]),
+            (mom_f_in, mom_f),
+            (mom_p_in, mom_p),
+            (mom_q_in, mom_q),
+            (mom_o_in, mom_o),
         ]
     ):
         copy = pltpu.make_async_copy(source, target, local_sem.at[which])
         copy.start()
         locals_.append(copy)
-    greet(("row", "col", "dp"))
 
     def halves(size):
         return rows_at(me_d, size // 2)
 
+    locals_[2].wait()
+    wq[me_r] = wq_own[...].T
     locals_[0].wait()
-    tok_z = wire.spread("col", lambda p: tok.at[me_r, own], lambda p: tok.at[me_r, own])
-    tok_r = [wire.spread("row", lambda p: tok.at[me_r, own], lambda p: tok.at[me_r, own])]
+    met()
+    tok_z = wire.spread("col", lambda p: tok.at[me_r, :, own], lambda p: tok.at[me_r, :, own])
+    tok_r = [wire.spread("row", lambda p: tok.at[me_r, :, own], lambda p: tok.at[me_r, :, own])]
     locals_[1].wait()
     vec_r = wire.spread("row", lambda p: vecs.at[me_r], lambda p: vecs.at[me_r])
-    locals_[2].wait()
     wq_half = halves(wq.shape[1])
     wq_r = wire.spread("row", lambda p: wq.at[me_r, wq_half], lambda p: wq.at[me_r, wq_half])
     locals_[3].wait()
-    grad_z = wire.spread("col", lambda p: grad_cols.at[own], lambda p: grad_cols.at[own])
+    grad_z = wire.spread("col", lambda p: grad_cols.at[:, own], lambda p: grad_cols.at[:, own])
     locals_[4].wait()
     wo_half = halves(wo.shape[2])
     wo_z = wire.spread(
         "col", lambda p: wo.at[me_c, me_r, wo_half], lambda p: wo.at[me_c, me_r, wo_half]
     )
 
+    span = 3 * HD
     for group in range(heads):
-        width = 3 * HD
-        bias_col[group * width : (group + 1) * width] = column_of(
-            bias_q[:, group * width : (group + 1) * width]
-        )
+        here = slice(group * span, (group + 1) * span)
+        bias_col[here] = column_of(bias_q[:, here])
     seg = seg_row[...].astype(wide)
     for turn in range(cols):
         here = slice(turn * block, (turn + 1) * block)
@@ -309,56 +318,60 @@
         tok_r.append(
             wire.spread(
                 "row",
-                lambda p, there=there: tok.at[me_r, there],
-                lambda p, there=there: tok.at[me_r, there],
+                lambda p, there=there: tok.at[me_r, :, there],
+                lambda p, there=there: tok.at[me_r, :, there],
             )
         )
     wq_s = []
     for step in range(1, rows):
         wq_r[step - 1].wait_recv()
         peer = lax.rem(me_r + rows - step, rows)
-        wq_s.append(wire.push(wq.at[peer, wq_half], wq.at[peer, wq_half], "dp", 1 - me_d))
+        wq_s.append(wire.push(wq.at[peer, wq_half], wq.at[peer, wq_half], "dp", other))
     arrived(wo_z)
     wo_r = wire.spread(
         "row", lambda p: wo.at[:, me_r, wo_half], lambda p: wo.at[:, me_r, wo_half]
     )
     arrived(grad_z)
     grad_r = wire.spread(
-        "row", lambda p: grad_cols.at[rows_at(p, block)], lambda p: grad_part.at[me_r]
+        "row",
+        lambda p: grad_cols.at[:, rows_at(p, block)],
+        lambda p: grad_turn.at[me_r],
     )
     locals_[5].wait()
     wf_half = halves(feats)
     wf_r = wire.spread("row", lambda p: wf.at[me_r, wf_half], lambda p: wf.at[me_r, wf_half])
     locals_[6].wait()
-    wp_half = halves(wp.shape[1])
-    wp_r = wire.spread("row", lambda p: wp.at[me_r, wp_half], lambda p: wp.at[me_r, wp_half])
-    grad_part[me_r] = grad_cols[part]
+    wp_r = wire.spread("row", lambda p: wp.at[me_r, wf_half], lambda p: wp.at[me_r, wf_half])
+    grad_turn[me_r] = grad_cols[:, part]
+    arrived(vec_r)
+    for slot in range(rows):
+        for which in range(2):
+            gains[slot, which] = column_of(vecs[slot, which : which + 1, :])
     for copies in tok_r:
         arrived(copies)
-    arrived(vec_r)
     arrived(wq_s)
 
     def norm_block(turn, carry):
         here = rows_at(turn, block)
-        values = [tok[slot, here, :].astype(wide) for slot in range(rows)]
-        mean = sum(jnp.sum(v, axis=1, keepdims=True) for v in values) / whole
-        square = sum(jnp.sum(v * v, axis=1, keepdims=True) for v in values) / whole
+        values = [tok[slot, :, here].astype(wide) for slot in range(rows)]
+        mean = sum(jnp.sum(v, axis=0, keepdims=True) for v in values) / whole
+        square = sum(jnp.sum(v * v, axis=0, keepdims=True) for v in values) / whole
         inv = lax.rsqrt(square - mean * mean + eps_norm)
-        mean_one[here] = mean
-        inv_one[here] = inv
+        mean_one[:, here] = mean
+        inv_one[:, here] = inv
         total_ = bias_col[...]
         for slot in range(rows):
             unit = (values[slot] - mean) * inv
-            act = (unit * vecs[slot, 0:1, :] + vecs[slot, 1:2, :]).astype(low)
-            act_one[slot, here, :] = act
-            total_ = total_ + contract(wq[slot], act, 1, 1)
+            act = (unit * gains[slot, 0] + gains[slot, 1]).astype(low)
+            act_one[slot, :, here] = act
+            total_ = total_ + contract(wq[slot], act, 1, 0)
         qkv[:, here] = total_.astype(low)
         return carry
 
     lax.fori_loop(0, cols, norm_block, 0)
 
     def forward_head(head, carry):
-        base = head * 3 * HD
+        base = head * span
         key = qkv[pl.ds(pl.multiple_of(base + HD, HD), HD), :]
         value = qkv[pl.ds(pl.multiple_of(base + 2 * HD, HD), HD), :]
         spot = rows_at(head, HD)
@@ -375,37 +388,36 @@
         return carry
 
     lax.fori_loop(0, heads, forward_head, 0)
-    attn_z = wire.spread(
-        "col", lambda p: attn.at[:, part], lambda p: attn_part.at[me_c]
-    )
+    attn_z = wire.spread("col", lambda p: attn.at[:, part], lambda p: attn_part.at[me_c])
     attn_part[me_c] = attn[:, part]
     arrived(wo_r)
     wo_s = []
     for step in range(1, rows):
         peer = lax.rem(me_r + rows - step, rows)
-        wo_s.append(wire.push(wo.at[:, peer, wo_half], wo.at[:, peer, wo_half], "dp", 1 - me_d))
+        wo_s.append(wire.push(wo.at[:, peer, wo_half], wo.at[:, peer, wo_half], "dp", other))
     for step in range(1, cols):
         peer = lax.rem(me_c + cols - step, cols)
-        wo_s.append(
-            wire.push(wo.at[peer, me_r, wo_half], wo.at[peer, me_r, wo_half], "dp", 1 - me_d)
-        )
+        wo_s.append(wire.push(wo.at[peer, me_r, wo_half], wo.at[peer, me_r, wo_half], "dp", other))
     wf_s, wp_s = [], []
     for step in range(1, rows):
         peer = lax.rem(me_r + rows - step, rows)
         wf_r[step - 1].wait_recv()
-        wf_s.append(wire.push(wf.at[peer, wf_half], wf.at[peer, wf_half], "dp", 1 - me_d))
+        wf_s.append(wire.push(wf.at[peer, wf_half], wf.at[peer, wf_half], "dp", other))
     for step in range(1, rows):
         peer = lax.rem(me_r + rows - step, rows)
         wp_r[step - 1].wait_recv()
-        wp_s.append(wire.push(wp.at[peer, wp_half], wp.at[peer, wp_half], "dp", 1 - me_d))
+        wp_s.append(wire.push(wp.at[peer, wf_half], wp.at[peer, wf_half], "dp", other))
+    arrived(grad_r)
+    for slot in range(rows):
+        grad_part[slot] = grad_turn[slot].T
+        mid[slot] = tok[slot, :, part].T.astype(wide) + vecs[slot, 4:5, :]
     arrived(wo_s)
-    arrived(grad_r)
     arrived(attn_z)
 
     turned = [attn_part[slot].T for slot in range(cols)]
     mids = []
     for slot in range(rows):
-        value = tok[slot, part, :].astype(wide) + vecs[slot, 4:5, :]
+        value = mid[slot]
         for across in range(cols):
             value = value + contract(turned[across], wo[across, slot], 1, 0)
         mid[slot] = value
@@ -425,7 +437,7 @@
     grad_hidden = None
     for slot in range(rows):
         pre = pre + contract(act_two[slot], wf[slot], 1, 0)
-        term = contract(grad_part[slot], wp[slot], 1, 1)
+        term = contract(grad_part[slot], wp[slot], 1, 0)
         grad_hidden = term if grad_hidden is None else grad_hidden + term
     curve = math.sqrt(2.0 / math.pi)
     square = pre * pre
@@ -447,22 +459,16 @@
     two_in[me_c] = two_out[:, bit, :]
     arrived(two_z)
 
-    two_sums, scaled, units = [], [], []
+    scaled, units = [], []
     for slot in range(rows):
         value = two_in[0, slot].astype(wide)
         for across in range(1, cols):
             value = value + two_in[across, slot].astype(wide)
         unit = unit_two[slot, bit, :]
-        two_sums.append(value)
         units.append(unit)
         scaled.append(value * vecs[slot, 2:3, :])
-        wide_out[slot] = jnp.concatenate(
-            [
-                jnp.sum(value * unit, axis=0, keepdims=True),
-                jnp.sum(value, axis=0, keepdims=True),
-            ],
-            axis=0,
-        )
+        wide_out[slot, 0:1] = jnp.sum(value * unit, axis=0, keepdims=True)
+        wide_out[slot, 1:2] = jnp.sum(value, axis=0, keepdims=True)
     first_mean = sum(jnp.sum(v, axis=1, keepdims=True) for v in scaled) / whole
     second_mean = (
         sum(jnp.sum(v * u, axis=1, keepdims=True) for v, u in zip(scaled, units)) / whole
@@ -483,25 +489,91 @@
     gattn[:, part] = value.astype(low)
     gattn_r = wire.spread("row", lambda p: gattn.at[:, part], lambda p: gattn.at[:, part])
     mid_r = wire.spread("row", lambda p: mid_part.at[p], lambda p: mid_cols.at[part])
-    resid_r = wire.spread("row", lambda p: mid.at[p], lambda p: resid_own.at[part])
     mid_cols[part] = mid_part[me_r]
-    resid_own[part] = mid[me_r]
+    wide_r = wire.spread("row", lambda p: wide_out.at[p], lambda p: wide_in.at[me_r])
+    wide_in[me_r] = wide_out[me_r]
+    giver = me_r == me_c
+    resid_r = []
+    base = wire.used
+    wire.used += rows
+    for step in range(1, rows):
+        peer = lax.rem(me_r + step, rows)
+        resid_r.append(
+            pltpu.make_async_remote_copy(
+                src_ref=mid.at[peer],
+                dst_ref=resid,
+                send_sem=send_sem.at[base + step],
+                recv_sem=recv_sem.at[base],
+                device_id={"row": peer},
+                device_id_type=pl.DeviceIdType.MESH,
+            )
+        )
+
+    @pl.when(giver)
+    def _():
+        for copy in resid_r:
+            copy.start()
+        resid[...] = mid[me_r]
 
     arrived(hid_r)
     arrived(gpre_r)
     arrived(act_r)
     sum_f[me_d] = contract(act_cols[...], gpre[...], 0, 0).astype(low)
-    pair = [wire.push(sum_f.at[me_d], sum_f.at[me_d], "dp", 1 - me_d)]
-    sum_p[me_d] = contract(hid[...], grad_cols[...], 0, 0).astype(low)
-    pair.append(wire.push(sum_p.at[me_d], sum_p.at[me_d], "dp", 1 - me_d))
+    pair_f = wire.push(sum_f.at[me_d], sum_f.at[me_d], "dp", other)
+    sum_p[me_d] = contract(grad_cols[...], hid[...], 1, 0).astype(low)
+    pair_p = wire.push(sum_p.at[me_d], sum_p.at[me_d], "dp", other)
     ones = jnp.ones((8, count), low)
     sum_bf[me_d] = contract(ones, gpre[...], 1, 0)
-    pair.append(wire.push(sum_bf.at[me_d], sum_bf.at[me_d], "dp", 1 - me_d))
-    outward[...] = contract(hid[...], wp[me_r], 1, 0).astype(low)
+    pair = [wire.push(sum_bf.at[me_d], sum_bf.at[me_d], "dp", other)]
+    outward[...] = contract(wp[me_r], hid[...], 1, 1).astype(low)
+    outward_z = wire.spread(
+        "col", lambda p: outward.at[:, rows_at(p, block)], lambda p: outward_in.at[me_c]
+    )
+    outward_in[me_c] = outward[:, own]
+
+    def push_of(sums, moment):
+        gradient = sums[0].astype(wide) + sums[1].astype(wide)
+        return (gradient + beta_mom * (beta_mom * moment[...] + gradient)).astype(low)
+
+    share = matrix.shape[1]
+    mine = rows_at(me_d, share)
+    push_r = []
+    base = wire.used
+    wire.used += rows
+    for step in range(1, rows):
+        peer = lax.rem(me_r + step, rows)
+        push_r.append(
+            pltpu.make_async_remote_copy(
+                src_ref=pushed.at[peer, :, mine],
+                dst_ref=matrix.at[rows_at(me_r, feats)],
+                send_sem=send_sem.at[base + step],
+                recv_sem=recv_sem.at[base + step],
+                device_id={"row": peer},
+                device_id_type=pl.DeviceIdType.MESH,
+            )
+        )
+
+    def launch(first, last):
+        for step in range(1, rows):
+            peer = lax.rem(me_r + step, rows)
+
+            @pl.when((peer >= first) & (peer < last))
+            def _(copy=push_r[step - 1]):
+                copy.start()
+
+    pushed[0] = jnp.zeros(pushed.shape[1:], low)
+    pushed[1] = jnp.zeros(pushed.shape[1:], low)
+    for which in range(7, 11):
+        locals_[which].wait()
+    pair_f.wait_recv()
+    pair_p.wait_recv()
+    pushed[2] = push_of(sum_f, mom_f)
+    pushed[3] = push_of(sum_p, mom_p)
+    launch(2, rows)
     arrived(gattn_r)
 
     def backward_head(head, carry):
-        base = head * 3 * HD
+        base = head * span
         spot_q = pl.ds(pl.multiple_of(base, HD), HD)
         spot_k = pl.ds(pl.multiple_of(base + HD, HD), HD)
         spot_v = pl.ds(pl.multiple_of(base + 2 * HD, HD), HD)
@@ -531,24 +603,195 @@
         return carry
 
     lax.fori_loop(0, heads, backward_head, 0)
-    sum_q[me_d] = contract(act_one[me_r], gqkv[...], 0, 1).astype(low)
-    pair.append(wire.push(sum_q.at[me_d], sum_q.at[me_d], "dp", 1 - me_d))
-    sum_bq[me_d] = contract(ones, gqkv[...], 1, 1)
-    pair.append(wire.push(sum_bq.at[me_d], sum_bq.at[me_d], "dp", 1 - me_d))
+    sum_q[me_d] = contract(act_one[me_r], gqkv[...], 1, 1).astype(low)
+    pair_q = wire.push(sum_q.at[me_d], sum_q.at[me_d], "dp", other)
     arrived(mid_r)
     sum_o[me_d] = contract(attn[...], mid_cols[...], 1, 0).astype(low)
-    pair.append(wire.push(sum_o.at[me_d], sum_o.at[me_d], "dp", 1 - me_d))
-    inward[...] = contract(gqkv[...], wq[me_r], 0, 0).astype(low)
-    mid_own[...] = mid_cols[own]
-    inv = inv_one[own]
-    inv_own[...] = inv
-    unit_own[...] = (tok[me_r, own].astype(wide) - mean_one[own]) * inv
-    arrived(resid_r)
+    pair_o = wire.push(sum_o.at[me_d], sum_o.at[me_d], "dp", other)
+    sum_bq[me_d] = contract(ones, gqkv[...], 1, 1)
+    pair.append(wire.push(sum_bq.at[me_d], sum_bq.at[me_d], "dp", other))
+    inward[...] = contract(wq_own[...], gqkv[...], 1, 0).astype(low)
+    inward_z = wire.spread(
+        "col", lambda p: inward.at[:, rows_at(p, block)], lambda p: inward_in.at[me_c]
+    )
+    inward_in[me_c] = inward[:, own]
+    pair_q.wait_recv()
+    pushed[0, :, : mom_q.shape[1]] = push_of(sum_q, mom_q)
+    pair_o.wait_recv()
+    pushed[1, :, : mom_o.shape[0]] = push_of(sum_o, mom_o).T
+    launch(0, 2)
+    matrix[rows_at(me_r, feats)] = pushed[me_r, :, mine]
+
+    arrived(outward_z)
+
+    @pl.when(jnp.logical_not(giver))
+    def _():
+        resid_r[0].wait_recv()
+
+    def slots_of(slots):
+        value = slots[0].astype(wide)
+        for across in range(1, slots.shape[0]):
+            value = value + slots[across].astype(wide)
+        return value
+
+    block_out[...] = (
+        resid[...].T + slots_of(outward_in) + column_of(vecs[me_r, 5:6, :])
+    ).astype(low)
+    arrived(inward_z)
+    grad_one = slots_of(inward_in)
+    inv = inv_one[:, own]
+    unit = (tok[me_r, :, own].astype(wide) - mean_one[:, own]) * inv
+    scaled_one = grad_one * gains[me_r, 0]
+    stat_out[0:1] = jnp.sum(scaled_one, axis=0, keepdims=True)
+    stat_out[1:2] = jnp.sum(scaled_one * unit, axis=0, keepdims=True)
+    stat_r = wire.spread("row", lambda p: stat_out, lambda p: stat_in.at[me_r])
+    stat_in[me_r] = stat_out[...]
+    arrived(wide_r)
+    wides = slots_of(wide_in)
+    term_out[...] = jnp.zeros_like(term_out)
+    term_out[0:1] = jnp.sum((grad_one * unit).T, axis=0, keepdims=True)
+    term_out[1:2] = jnp.sum(grad_one.T, axis=0, keepdims=True)
+    term_out[2:4] = wides
+    term_out[4:5] = jnp.sum(mid_cols[own].astype(wide), axis=0, keepdims=True)
+    term_out[5:6] = jnp.sum(grad_cols[:, own].astype(wide).T, axis=0, keepdims=True)
+
+    for copy in push_r:
+        copy.wait_recv()
+    edge = packed.shape[1]
+    bands = [matrix[up * edge : (up + 1) * edge] for up in range(3)]
+    spots = [(0, 0), (0, 1), (0, 2), (1, 1), (1, 2), (2, 2)]
+    for which, (up, across) in enumerate(spots):
+        packed[which] = contract(bands[up], bands[across], 1, 1).astype(low)
+    packed_s = wire.push(packed.at[rows_at(other, 3)], packed_in, "dp", other)
+    packed_s.wait_recv()
+    long = 3 * edge
+    halved[...] = (
+        (packed[rows_at(me_d, 3)].astype(wide) + packed_in[...].astype(wide))
+        .astype(low)
+        .reshape(long, edge)
+    )
+    fourth = long // cols
+    quarter = rows_at(me_c, fourth)
+    quarter_z = wire.spread(
+        "col", lambda p: halved.at[rows_at(p, fourth)], lambda p: quarter_in.at[me_c]
+    )
+    quarter_in[me_c] = halved[quarter]
+    term_z = wire.spread("col", lambda p: term_out, lambda p: term_in.at[me_c])
+    term_in[me_c] = term_out[...]
+    arrived(stat_r)
+    stats = slots_of(stat_in) / whole
+    input_grad[...] = mid_cols[own].astype(wide).T + inv_one[:, own] * (
+        scaled_one - stats[0:1] - unit * stats[1:2]
+    )
+    arrived(quarter_z)
+    gathered[me_d, quarter] = slots_of(quarter_in).astype(low)
+    whole_z = wire.spread(
+        "col", lambda p: gathered.at[me_d, quarter], lambda p: gathered.at[me_d, quarter]
+    )
+    whole_s = [wire.push(gathered.at[me_d, quarter], gathered.at[me_d, quarter], "dp", other)]
+    arrived(term_z)
+    term_pair[me_d] = slots_of(term_in)
+    term_s = wire.push(term_pair.at[me_d], term_pair.at[me_d], "dp", other)
+    for step in range(1, cols):
+        whole_z[step - 1].wait_recv()
+        there = rows_at(lax.rem(me_c + cols - step, cols), fourth)
+        whole_s.append(
+            wire.push(gathered.at[me_d, there], gathered.at[me_d, there], "dp", other)
+        )
+    arrived(whole_s)
+    square = None
+    for which, (up, across) in enumerate(spots):
+        at = which % 3 * edge
+        tile = gathered[which // 3, at : at + edge].astype(wide)
+        gram[up * edge : (up + 1) * edge, across * edge : (across + 1) * edge] = tile
+        power = jnp.sum(jnp.sum(tile * tile, axis=0, keepdims=True), axis=1, keepdims=True)
+        if across > up:
+            gram[across * edge : (across + 1) * edge, up * edge : (up + 1) * edge] = tile.T
+            power = power + power
+        square = power if square is None else square + power
+    gram_norm = jnp.sqrt(square) + eps_gram
+    now = gram[...] * (1.0 / gram_norm)
+    now_low = now.astype(low)
+    poly = (coef_b * now + coef_c * contract(now_low, now_low, 1, 0)).astype(low)
+    held = coef_a * now + contract(poly, now_low, 1, 0)
+    moved = coef_a * matrix[...].astype(wide) + contract(poly, matrix[...], 1, 0)
+    now = coef_a * held + contract(held.astype(low), poly, 1, 0)
+    now_low = now.astype(low)
+    poly = (coef_b * now + coef_c * contract(now_low, now_low, 1, 0)).astype(low)
+    moved = coef_a * moved + contract(poly, moved.astype(low), 1, 0)
+    ortho[...] = (moved * lax.rsqrt(gram_norm)).astype(low)
+    back_r = wire.spread(
+        "row", lambda p: ortho.at[rows_at(p, feats)], lambda p: back.at[me_d, me_r]
+    )
+    back[me_d, me_r] = ortho[rows_at(me_r, feats)]
+    back_s = [wire.push(back.at[me_d, me_r], back.at[me_d, me_r], "dp", other)]
+    term_s.wait_recv()
+    grad_rows[...] = term_pair[0] + term_pair[1]
     arrived(pair)
+    for step in range(1, rows):
+        back_r[step - 1].wait_recv()
+        peer = lax.rem(me_r + rows - step, rows)
+        back_s.append(wire.push(back.at[me_d, peer], back.at[me_d, peer], "dp", other))
+    arrived(back_s)
+    for copy in push_r:
+        copy.wait_send()
+
+    @pl.when(giver)
+    def _():
+        for copy in resid_r:
+            copy.wait_send()
+
     wire.drain()
 
 
-def front(tokens, out_grad, segment_ids, w_qkv, w_out, w_fc, w_proj, bias_qkv, bias_fc, row_vectors):
+def last_kernel(rate, vector_rate, *refs):
+    wide = jnp.float32
+    (
+        sum_q, sum_o, sum_f, sum_p, sum_bq, sum_bf, block_in, input_in, rows_in, back,
+        w_q, w_o, w_f, w_p, bias_q, bias_f, vectors, mom_q, mom_o, mom_f, mom_p, mom_bq, mom_bf,
+        mom_rows,
+        block_out, input_grad, grad_q, grad_o, grad_f, grad_p, grad_bq, grad_bf, grad_rows,
+        new_q, new_o, new_f, new_p, new_bq, new_bf, new_rows,
+        next_q, next_o, next_f, next_p, next_bq, next_bf, next_rows,
+    ) = refs
+    block_out[...] = block_in[...]
+    input_grad[...] = input_in[...]
+    share = back.shape[3]
+    members = (
+        (sum_q, w_q, mom_q, grad_q, new_q, next_q, False),
+        (sum_o, w_o, mom_o, grad_o, new_o, next_o, True),
+        (sum_f, w_f, mom_f, grad_f, new_f, next_f, False),
+        (sum_p, w_p, mom_p, grad_p, new_p, next_p, False),
+    )
+    for member, (sums, weight, moment, gradient, new, later, flip) in enumerate(members):
+        value = sums[0].astype(wide) + sums[1].astype(wide)
+        gradient[...] = value
+        later[...] = beta_mom * moment[...] + value
+        width = weight.shape[1]
+        for start in range(0, width, share):
+            stop = min(start + share, width)
+            turn = back[start // share, member, :, : stop - start].astype(wide)
+            if flip:
+                turn = turn.T
+            here = (slice(None), slice(start, stop))
+            new[here] = weight[here].astype(wide) - rate[member] * turn
+    vector_members = (
+        (sum_bq[0, 0:1] + sum_bq[1, 0:1], bias_q, mom_bq, grad_bq, new_bq, next_bq),
+        (sum_bf[0, 0:1] + sum_bf[1, 0:1], bias_f, mom_bf, grad_bf, new_bf, next_bf),
+        (rows_in[: vectors.shape[0]], vectors, mom_rows, grad_rows, new_rows, next_rows),
+    )
+    for value, weight, moment, gradient, new, later in vector_members:
+        value = value.reshape(gradient.shape)
+        new_moment = beta_mom * moment[...] + value
+        gradient[...] = value
+        later[...] = new_moment
+        new[...] = weight[...] - vector_rate * (value + beta_mom * new_moment)
+
+
+def paired_local(
+    tokens, out_grad, segment_ids, w_qkv, w_out, w_fc, w_proj, bias_qkv, bias_fc, row_vectors,
+    mom_qkv, mom_out, mom_fc, mom_proj, mom_bias_qkv, mom_bias_fc, mom_rows,
+):
     low, wide = jnp.bfloat16, jnp.float32
     rows, cols = lax.axis_size("row"), lax.axis_size("col")
     block, feats = tokens.shape
@@ -556,34 +799,41 @@
     piece = block // cols
     width, hidden = w_qkv.shape[1], w_fc.shape[1]
     heads = width // (3 * HD)
+    whole = feats * rows
+    edge = whole // 3
+    share = max(width, hidden, w_out.shape[0]) // 2
+    lines = row_vectors.shape[0]
+    assert rows == 4 and w_out.shape[0] <= share < width <= 2 * share
     shape = jax.ShapeDtypeStruct
+    loose = pl.BlockSpec(memory_space=pl.ANY)
+    near = pl.BlockSpec(memory_space=pltpu.VMEM)
     outs = [
         shape((2, feats, width), low),
         shape((2, w_out.shape[0], feats), low),
         shape((2, feats, hidden), low),
-        shape((2, hidden, feats), low),
+        shape((2, feats, hidden), low),
         shape((2, 8, width), wide),
         shape((2, 8, hidden), wide),
-        shape((count, feats), low),
-        shape((count, feats), low),
-        shape((block, feats), wide),
-        shape((block, 1), wide),
-        shape((block, feats), low),
-        shape((count, feats), wide),
-        shape((rows, 2, feats), wide),
+        shape((feats, block), low),
+        shape((feats, block), wide),
+        shape((8, feats), wide),
+        shape((2, rows, feats, share), low),
     ]
     buffers = [
-        ((rows, count, feats), low),
-        ((count, feats), low),
+        ((rows, feats, count), low),
+        ((feats, count), low),
+        ((rows, feats, block), low),
         ((rows, block, feats), low),
-        ((rows, row_vectors.shape[0], feats), wide),
+        ((rows, lines, feats), wide),
+        ((feats, width), low),
         ((rows, width, feats), low),
         ((cols, rows, w_out.shape[0], feats), low),
         ((rows, feats, hidden), low),
-        ((rows, hidden, feats), low),
-        ((rows, count, feats), low),
+        ((rows, feats, hidden), low),
+        ((rows, feats, count), low),
         ((width, count), low),
         ((width, 1), wide),
+        ((rows, 2, feats, 1), wide),
         ((count, count), wide),
         ((heads, count, count), wide),
         ((heads * HD, count), low),
@@ -593,6 +843,7 @@
         ((rows, block, feats), low),
         ((count, feats), low),
         ((rows, block, feats), wide),
+        ((block, feats), wide),
         ((count, hidden), low),
         ((count, hidden), low),
         ((rows, block, feats), low),
@@ -604,35 +855,98 @@
         ((width, count), low),
         ((HD, count), wide),
         ((HD, count), wide),
-        ((count, 1), wide),
-        ((count, 1), wide),
+        ((1, count), wide),
+        ((1, count), wide),
+        ((rows, 2, feats), wide),
+        ((rows, 2, feats), wide),
+        ((feats, count), low),
+        ((cols, feats, block), low),
+        ((feats, count), low),
+        ((cols, feats, block), low),
+        ((2, block), wide),
+        ((rows, 2, block), wide),
+        ((8, feats), wide),
+        ((cols, 8, feats), wide),
+        ((2, 8, feats), wide),
+        (mom_qkv.shape, wide),
+        (mom_out.shape, wide),
+        (mom_fc.shape, wide),
+        (mom_proj.shape[::-1], wide),
+        ((rows, feats, 2 * share), low),
+        ((whole, share), low),
+        ((6, edge, edge), low),
+        ((3, edge, edge), low),
+        ((whole, edge), low),
+        ((cols, whole // cols, edge), low),
+        ((2, whole, edge), low),
+        ((whole, whole), wide),
+        ((whole, share), low),
     ]
-    loose = pl.BlockSpec(memory_space=pl.ANY)
-    near = pl.BlockSpec(memory_space=pltpu.VMEM)
-    return pl.pallas_call(
-        front_kernel,
+    middle = pl.pallas_call(
+        step_kernel,
         out_shape=outs,
-        in_specs=[loose, loose, near, loose, loose, loose, loose, near, near, loose],
+        in_specs=[loose, loose, near, loose, loose, loose, loose, near, near] + [loose] * 5,
         out_specs=[near] * len(outs),
         scratch_shapes=[pltpu.VMEM(size, kind) for size, kind in buffers]
         + [
-            pltpu.SemaphoreType.DMA((front_wires,)),
-            pltpu.SemaphoreType.DMA((front_wires,)),
-            pltpu.SemaphoreType.DMA((7,)),
+            pltpu.SemaphoreType.DMA((step_wires,)),
+            pltpu.SemaphoreType.DMA((step_wires,)),
+            pltpu.SemaphoreType.DMA((11,)),
         ],
         compiler_params=pltpu.CompilerParams(collective_id=20, has_side_effects=True),
     )(
-        tokens,
-        out_grad,
+        tokens.T,
+        out_grad.T,
         segment_ids,
-        w_qkv.T,
+        w_qkv,
         w_out,
         w_fc,
-        w_proj,
+        w_proj.T,
         bias_qkv[None],
         bias_fc[None],
         row_vectors,
-    )
+        mom_qkv,
+        mom_out,
+        mom_fc,
+        mom_proj.T,
+    )
+    longest = [
+        max(whole, width * cols),
+        max(whole, w_out.shape[0] * cols),
+        max(whole, hidden * cols),
+        max(whole, hidden * cols),
+    ]
+    rate = tuple(rate_matrix * math.sqrt(size) for size in longest)
+    matrices = [w_qkv.shape, w_out.shape, w_fc.shape, w_proj.shape[::-1]]
+    vectors = [bias_qkv.shape, bias_fc.shape, row_vectors.shape]
+    group = [shape(size, wide) for size in matrices + vectors]
+    results = list(
+        pl.pallas_call(
+            functools.partial(last_kernel, rate, rate_vector / math.sqrt(count * 2)),
+            out_shape=[shape((feats, block), low), shape((feats, block), wide)] + group * 3,
+            in_specs=[near] * 24,
+            out_specs=[near] * 23,
+        )(
+            *middle,
+            w_qkv,
+            w_out,
+            w_fc,
+            w_proj.T,
+            bias_qkv,
+            bias_fc,
+            row_vectors,
+            mom_qkv,
+            mom_out,
+            mom_fc,
+            mom_proj.T,
+            mom_bias_qkv,
+            mom_bias_fc,
+            mom_rows,
+        )
+    )
+    for which in (0, 1, 5, 12, 19):
+        results[which] = results[which].T
+    return tuple(results)
 
 
 def local(
@@ -926,223 +1240,6 @@
             wide_sum[0],
             wide_sum[1],
             jnp.sum(own_rows(mid_cols), axis=0, dtype=jnp.float32),
-            jnp.sum(out_grad, axis=0, dtype=jnp.float32),
-        ]
-    )
-    quarter_slots, term_slots = exchange(
-        "col",
-        [gram_half.reshape(col_parts, -1, edge), row_terms],
-        [True, False],
-        9,
-    )
-    (whole_slots,) = exchange("col", [total(quarter_slots).astype(low)], [False], 10)
-    gram_half = whole_slots.reshape(gram_half.shape)
-    if dp_parts == 2:
-        gram_slots, pair_slots = exchange(
-            "dp", [gram_half, total(term_slots)], [False, False], 11
-        )
-        gram_half = gram_slots
-    else:
-        (pair_slots,) = exchange("dp", [total(term_slots)], [False], 11)
-    grad_rows = total(pair_slots)
-    tiles = gram_half.reshape(len(spots), edge, edge)
-    found = {spot: tiles[which] for which, spot in enumerate(spots)}
-    gram = jnp.concatenate(
-        [
-            jnp.concatenate(
-                [
-                    found[up, across] if across >= up else found[across, up].T
-                    for across in range(3)
-                ],
-                axis=1,
-            )
-            for up in range(3)
-        ],
-        axis=0,
-    ).astype(jnp.float32)
-    factor, scale, gram_norm = polynomial_factor(gram)
-    ortho = (scale * matrix.astype(jnp.float32) + matrix_product(factor, matrix)) * lax.rsqrt(
-        gram_norm
-    )
-    (back,) = exchange(
-        "row", [ortho.astype(low).reshape(row_parts, own_features, share)], [True], 12
-    )
-    if dp_parts == 2:
-        (ortho_slots,) = exchange("dp", [back], [False], 13)
-        orthos = jnp.concatenate([ortho_slots[part] for part in range(dp_parts)], axis=2)
-    else:
-        orthos = lax.all_gather(back, "dp", axis=2, tiled=True)
-    new_weights = []
-    for member in range(4):
-        piece = orthos[member, :, : upright[member].shape[1]]
-        if flips[member]:
-            piece = piece.T
-        longest = max(
-            upright[member].shape[0] * row_parts, upright[member].shape[1] * col_parts
-        )
-        new_weights.append(
-            weights[member].astype(jnp.float32)
-            - rate_matrix * math.sqrt(longest) * piece.astype(jnp.float32)
-        )
-
-    vector_rate = rate_vector / math.sqrt(token_count * dp_parts)
-
-    def vector_step(weight, gradient, moment):
-        new_moment = beta_mom * moment + gradient
-        return (weight - vector_rate * (gradient + beta_mom * new_moment), new_moment)
-
-    new_bias_qkv, new_mom_bias_qkv = vector_step(bias_qkv, summed[4], mom_bias_qkv)
-    new_bias_fc, new_mom_bias_fc = vector_step(bias_fc, summed[5], mom_bias_fc)
-    new_rows, new_mom_rows = vector_step(row_vectors, grad_rows, mom_rows)
-    return (
-        block_out,
-        input_grad,
-        summed[0],
-        summed[1],
-        summed[2],
-        summed[3],
-        summed[4],
-        summed[5],
-        grad_rows,
-        new_weights[0],
-        new_weights[1],
-        new_weights[2],
-        new_weights[3],
-        new_bias_qkv,
-        new_bias_fc,
-        new_rows,
-        new_moms[0],
-        new_moms[1],
-        new_moms[2],
-        new_moms[3],
-        new_mom_bias_qkv,
-        new_mom_bias_fc,
-        new_mom_rows,
-    )
-
-
-def paired_local(
-    tokens,
-    out_grad,
-    segment_ids,
-    w_qkv,
-    w_out,
-    w_fc,
-    w_proj,
-    bias_qkv,
-    bias_fc,
-    row_vectors,
-    mom_qkv,
-    mom_out,
-    mom_fc,
-    mom_proj,
-    mom_bias_qkv,
-    mom_bias_fc,
-    mom_rows,
-):
-    low = jnp.bfloat16
-    score_scale = 1.0 / math.sqrt(HD)
-    row_parts = lax.axis_size("row")
-    col_parts = lax.axis_size("col")
-    dp_parts = lax.axis_size("dp")
-    own_tokens, own_features = tokens.shape
-    token_count = own_tokens * col_parts
-    feature_count = own_features * row_parts
-    token_base = lax.axis_index("col") * own_tokens
-    feature_base = lax.axis_index("row") * own_features
-
-    def own_columns(whole):
-        return lax.dynamic_slice_in_dim(whole, feature_base, own_features, 1)
-
-    def own_block(whole):
-        return lax.dynamic_slice(whole, (token_base, feature_base), (own_tokens, own_features))
-
-    def own_rows(whole):
-        return lax.dynamic_slice_in_dim(whole, token_base, own_tokens, 0)
-
-    proj_flip = w_proj.T
-    (
-        slots_q, slots_o, slots_f, slots_p, slots_bq, slots_bf, outward, inward, unit_one_own,
-        inv_own, mid_own, resid_all, wide_terms,
-    ) = front(
-        tokens, out_grad, segment_ids, w_qkv, w_out, w_fc, w_proj, bias_qkv, bias_fc, row_vectors
-    )
-    resid_own = own_rows(resid_all)
-    summed = [total(slots) for slots in (slots_q, slots_o, slots_f, slots_p)]
-    summed = summed + [total(slots_bq)[0], total(slots_bf)[0]]
-
-    weights = (w_qkv, w_out, w_fc, w_proj)
-    moments = (mom_qkv, mom_out, mom_fc, mom_proj)
-    flips = (False, True, False, True)
-    new_moms = [beta_mom * moments[member] + summed[member] for member in range(4)]
-    pushes = [
-        (summed[member] + beta_mom * new_moms[member]).astype(low) for member in range(4)
-    ]
-    upright = [pushes[member].T if flips[member] else pushes[member] for member in range(4)]
-    widest = max(piece.shape[1] for piece in upright)
-    share = -(-widest // dp_parts)
-    assert row_parts == len(upright)
-    outgoing = jnp.stack(
-        [
-            jnp.pad(piece, ((0, 0), (0, share * dp_parts - piece.shape[1])))
-            for piece in upright
-        ]
-    )
-    outgoing = lax.dynamic_slice_in_dim(outgoing, lax.axis_index("dp") * share, share, 2)
-    arrived, block_slots, one_slots = exchange(
-        ["row", "col", "col"],
-        [
-            outgoing,
-            outward.reshape(col_parts, own_tokens, own_features),
-            inward.reshape(col_parts, own_tokens, own_features),
-        ],
-        [True] * 3,
-        7,
-    )
-    matrix = arrived.reshape(feature_count, share)
-    gram_low = product(matrix, matrix, True).astype(low)
-    edge = feature_count // 3
-    spots = [(0, 0), (0, 1), (0, 2), (1, 1), (1, 2), (2, 2)]
-    packed = jnp.concatenate(
-        [
-            gram_low[up * edge : (up + 1) * edge, across * edge : (across + 1) * edge]
-            for up, across in spots
-        ],
-        axis=0,
-    )
-    block_out = (resid_own + total(block_slots) + row_vectors[5]).astype(low)
-    grad_norm_one = total(one_slots)
-    scaled_one = grad_norm_one * row_vectors[0]
-    stat_pair = jnp.stack(
-        [jnp.sum(scaled_one, axis=1), jnp.sum(scaled_one * unit_one_own, axis=1)]
-    )
-    wide_slot_terms = wide_terms
-    if dp_parts == 2:
-        stat_slots, wide_slots, half_slots = exchange(
-            ["row", "row", "dp"],
-            [stat_pair, wide_slot_terms, packed.reshape(dp_parts, -1, edge)],
-            [False, True, True],
-            8,
-        )
-        gram_half = total(half_slots).astype(low)
-    else:
-        stat_slots, wide_slots = exchange(
-            "row", [stat_pair, wide_slot_terms], [False, True], 8
-        )
-        gram_half = lax.psum(packed, "dp")
-    stat_sum = total(stat_slots)
-    first_sum, second_sum = stat_sum[0][:, None], stat_sum[1][:, None]
-    wide_sum = total(wide_slots)
-    input_grad = mid_own.astype(jnp.float32) + inv_own * (
-        scaled_one - first_sum / feature_count - unit_one_own * (second_sum / feature_count)
-    )
-    row_terms = jnp.stack(
-        [
-            jnp.sum(grad_norm_one * unit_one_own, axis=0),
-            jnp.sum(grad_norm_one, axis=0),
-            wide_sum[0],
-            wide_sum[1],
-            jnp.sum(mid_own, axis=0, dtype=jnp.float32),
             jnp.sum(out_grad, axis=0, dtype=jnp.float32),
         ]
     )

time: 217 us -> 138 us (0.64); the launches traced: 214 us -> 137 us
  Pallas kernels: 157 us -> 134 us
  other arithmetic: 22.5 us -> 0 us
  local copies, waits for them, and re-layouts: 20 us -> 2.53 us
  matrix products: 13 us -> 0 us
    pallas_call x8 -> x2, Pallas kernels: 157 us -> 134 us  [the longest x1 128 us: paired_local(): pl.pallas_call(step_kernel, out_shape=outs, in_specs=[loose, loose, near,...]
    dot_general x6 -> x0, matrix products: 13 us -> none  [the longest x5 10.9 us: matrix_product(): jnp.dot(left_side.astype(jnp.bfloat16), right_side.astype(jnp.bfloat16),...]
    unnamed x85 -> x0, local copies, waits for them, and re-layouts: 12.3 us -> none
    reduce_sum x18 -> x0, other arithmetic: 11.7 us -> none  [the longest x13 8.14 us: total(): return jnp.sum(slots.astype(jnp.float32), axis=0)]
    another operation x4 -> x0, other arithmetic: 4.66 us -> none  [the longest x3 4.09 us: paired_local(): jnp.stack([jnp.pad(piece, ((0, 0), (0, share * dp_parts - piece.shape[1])...]
    sub x7 -> x0, other arithmetic: 4.47 us -> none  [the longest x4 2.66 us: paired_local(): weights[member].astype(jnp.float32)]
    slice x4 -> x0, local copies, waits for them, and re-layouts: 2.48 us -> none  [the longest x1 1.27 us: paired_local(): found = {spot: tiles[which] for which, spot in enumerate(spots)}]
where the time goes in v2:
time: 138 us; the launch traced here: 137 us
  Pallas kernels  134 us (97%)
  local copies, waits for them, and re-layouts  2.53 us (2%)
    pallas_call x1, Pallas kernels, paired_local(): pl.pallas_call(step_kernel, out_shape=outs, in_specs=[loose, loose, near,...  128 us
    pallas_call x1, Pallas kernels, paired_local(): pl.pallas_call(functools.partial(last_kernel, rate, rate_vector / math.sq...  5.6 us

profile of v2, /device:TPU:25, one launch (start us, length us, event | category | flops | bytes accessed | tf_op | source)
XLA Modules:
  0.0 137.4 jit_solution(14849348366641447632)
XLA Ops:
  0.7 1.3 broadcast_in_dim.6.refs_7_
  1.9 1.3 broadcast_in_dim.7.refs_8_
  3.2 128.4 %shard_map.344 = (bf16[2,192,576]{2,1,0:T(8,128)(2,1)}, bf16[2,192,192]{2,1,0:T(8,128)(2,1)}, bf16[2,192,768]{2,1,0:T(8,128)(2,1)}, bf16[2,192,768]{2,1,0:T(8,12...) custom-call(bf16[192,128]{1,0:T(8,128)(2,1)} %bitcast.13, ...), custom_call_target="tpu_custom_call" | custom-call | tf_op jit(solution)/shard_map/pallas_call | solution.py:885
  131.6 5.6 %shard_map.345 = (bf16[192,128]{1,0:T(8,128)(2,1)}, f32[192,128]{1,0:T(8,128)}, f32[192,576]{1,0:T(8,128)}, f32[192,192]{1,0:T(8,128)}, f32[192,768]{1,0:T(8,128...) custom-call(bf16[2,192,576]{2,1,0:T(8,128)(2,1)} %get-tuple-element., ...), custom_call_target="tpu_custom_call" | custom-call | tf_op jit(solution)/shard_map/pallas_call | solution.py:924
